TPU v7x, 32 devices: a whole 2x2x4 slice. The times are simulated.
32 devices in a mesh: group: 2 (over y), head: 8 (over z, x), dp: 2 (over core).
Axes of the slice: x: 2, y: 2, z: 4, core: 2. Of those that a mesh axis runs over, the one named last changes fastest.
Arguments:
- queries: bfloat16 [32, 16384], P(('group', 'dp'), 'head'), parts along dimension 0, may hold values from -6 to 6
- new_kv: bfloat16 [32, 2, 1024], P(('group', 'dp')), parts along dimension 0, may hold values from -6 to 6
- positions: int32 [32], P(('group', 'dp')), parts along dimension 0, may hold values from 256 to 1023
- lengths: int32 [32], P(('group', 'dp')), parts along dimension 0, may hold values from 2 to 256, as said below
- kv_codes: bfloat16 [32, 2, 256, 1024], P(('group', 'dp'), None, 'head'), parts along dimension 0, may hold values from -8 to 7, as said below
- kv_scales: float32 [32, 2, 8, 256], P(('group', 'dp'), None, None, 'head'), parts along dimension 0, may hold values from 0.1 to 40
- wo_codes: bfloat16 [16384, 16384], P('head'), may hold values from -8 to 7, as said below
- wo_scales: float32 [16384], P('head'), may hold values from 0.004 to 0.03
- residual: bfloat16 [32, 16384], P(('group', 'dp'), 'head'), parts along dimension 0, may hold values from -6 to 6
Outputs:
- hidden_out: bfloat16 [32, 16384], P(('group', 'dp'), 'head'), parts along dimension 0
There are 2 independent parts, one for each index of `group`. A program takes and returns all parts, laid end to end along the dimension named above; an argument that names none is the same for every part. Nothing has to cross between parts.
Inputs may be any that keep to these rules, and one draw needn't show every extreme that they name: Each row has at least two live slots, which are slots 0 to lengths - 1 of every key-value head; some row is full (256 live slots). `kv_codes`: integer codes. `wo_codes`: integer codes.
All inputs are finite; a program needn't handle non-finite values.
Results may differ from a plain program's by a relative error of at most 0.0089.
Values may be sent and summed in bfloat16 or wider, within the bound.
No kernel may reach another device: no remote copies, remote signals or barrier semaphores. Data moves between devices by JAX's collectives and lax.ppermute only.
A program may use at most 128 MiB of HBM per device.

v0:
```python
import jax
import jax.numpy as jnp
from jax import lax
from jax.sharding import PartitionSpec as P

H = 128
KVH = 8
HD = 128


ROPE_BASE = 500000.0
NEG_FILL = -1e30


def partner_2(block, axis, distance):
    count = lax.axis_size(axis)
    route = []
    for low in range(count):
        high = low | 1 << distance
        if high != low and high < count:
            route += [(low, high), (high, low)]
    return lax.ppermute(block, axis, route)


def rotary(values_in, positions):
    half_dim = values_in.shape[-1] // 2
    inverse_rate = ROPE_BASE ** (
        -(jnp.arange(half_dim, dtype=jnp.float32) * (2.0 / values_in.shape[-1]))
    )
    angles = positions.astype(jnp.float32)[:, None, None] * inverse_rate
    cosine = jnp.cos(angles)
    sine_part = jnp.sin(angles)
    lower_half = values_in[..., :half_dim]
    upper_half = values_in[..., half_dim:]
    return jnp.concatenate(
        [
            lower_half * cosine - upper_half * sine_part,
            upper_half * cosine + lower_half * sine_part,
        ],
        axis=-1,
    )


def hadamard(size_needed):
    index_row = jnp.arange(size_needed, dtype=jnp.int32)
    common = jnp.bitwise_and(index_row[:, None], index_row[None, :])
    parity = jnp.zeros_like(common)
    for bit_pos in range(max(size_needed.bit_length() - 1, 0)):
        parity = parity + jnp.right_shift(common, bit_pos) % 2
    return jnp.where(parity % 2 == 0, 1.0, -1.0).astype(jnp.float32)


def settle(peak_source, total_source, summed_source, fresh_score, fresh_values):
    peak_final = jnp.maximum(jnp.max(peak_source, axis=1), fresh_score)
    rescale = jnp.exp(peak_source - peak_final[:, None])
    fresh_weight = jnp.exp(fresh_score - peak_final)
    total_final = jnp.sum(total_source * rescale, axis=1) + fresh_weight
    summed_final = (
        jnp.sum(summed_source * rescale[..., None], axis=1) + fresh_weight[..., None] * fresh_values
    )
    return (summed_final / total_final[..., None]).astype(jnp.bfloat16)


def on_device(
    queries, new_kv, positions, lengths, kv_codes, kv_scales, wo_codes, wo_scales, residual
):
    n_head = lax.axis_size("head")
    my_index = lax.axis_index("head")
    n_rows = queries.shape[0]
    heads_here = queries.shape[1] // HD
    group_size = H // KVH
    block_len = kv_codes.shape[2]
    first_slot = my_index * block_len
    score_scale = HD ** (-0.5)
    own_query = rotary(
        queries.reshape(n_rows, heads_here, HD).astype(jnp.float32), positions
    ).astype(jnp.bfloat16)
    all_query = lax.all_gather(
        own_query.reshape(n_rows, heads_here * HD), "head", axis=1, tiled=True
    )
    all_query = all_query.reshape(n_rows, KVH, group_size, HD)
    fresh_keys = rotary(
        new_kv[:, 0].reshape(n_rows, KVH, HD).astype(jnp.float32), positions
    ).astype(jnp.bfloat16)
    fresh_values = new_kv[:, 1].reshape(n_rows, KVH, HD).astype(jnp.float32)
    key_codes = kv_codes[:, 0].reshape(n_rows, block_len, KVH, HD)
    value_codes = kv_codes[:, 1].reshape(n_rows, block_len, KVH, HD).astype(jnp.float32)
    raw_scores = jnp.einsum(
        "rgjd,rtgd->rgjt", all_query, key_codes, preferred_element_type=jnp.float32
    )
    scores = raw_scores * kv_scales[:, 0][:, :, None, :] * score_scale
    slot_index = first_slot + jnp.arange(block_len, dtype=jnp.int32)
    is_valid = (slot_index[None, :] < lengths[:, None])[:, None, None, :]
    scores = jnp.where(is_valid, scores, NEG_FILL)
    peak_here = jnp.max(scores, axis=-1)
    weights = jnp.where(is_valid, jnp.exp(scores - peak_here[..., None]), 0.0)
    total_here = jnp.sum(weights, axis=-1)
    summed = jnp.einsum(
        "rgjt,rtgd->rgjd",
        weights * kv_scales[:, 1][:, :, None, :],
        value_codes,
        precision=lax.Precision.HIGHEST,
    )
    peak_full = peak_here.reshape(n_rows, H)
    total_full = total_here.reshape(n_rows, H)
    summed_full = summed.reshape(n_rows, H, HD)
    received = (
        lax.all_to_all(peak_full, "head", split_axis=1, concat_axis=1, tiled=True),
        lax.all_to_all(total_full, "head", split_axis=1, concat_axis=1, tiled=True),
        lax.all_to_all(summed_full, "head", split_axis=1, concat_axis=1, tiled=True),
    )
    peak_source = received[0].reshape(n_rows, n_head, heads_here)
    total_source = received[1].reshape(n_rows, n_head, heads_here)
    summed_source = received[2].reshape(n_rows, n_head, heads_here, HD)
    owned_group = my_index * heads_here // group_size
    key_owned = lax.dynamic_index_in_dim(fresh_keys, owned_group, 1, keepdims=False)
    fresh_score = (
        jnp.einsum("rjd,rd->rj", own_query, key_owned, preferred_element_type=jnp.float32)
        * score_scale
    )
    value_owned = lax.dynamic_index_in_dim(fresh_values, owned_group, 1, keepdims=False)
    fresh_spread = jnp.broadcast_to(value_owned[:, None, :], (n_rows, heads_here, HD))
    attended = settle(peak_source, total_source, summed_source, fresh_score, fresh_spread)
    local_table = hadamard(heads_here)
    rotated = jnp.einsum(
        "kj,rjd->rkd", local_table, attended.astype(jnp.float32), precision=lax.Precision.HIGHEST
    )
    for bit_pos in range(n_head.bit_length() - 1):
        partner = partner_2(rotated, "head", bit_pos)
        is_upper = jnp.right_shift(my_index, bit_pos) % 2 == 1
        rotated = jnp.where(is_upper, partner - rotated, rotated + partner)
    flat_rows = (rotated * H ** (-0.5)).reshape(n_rows, heads_here * HD).astype(jnp.bfloat16)
    partial_out = jnp.dot(flat_rows, wo_codes, preferred_element_type=jnp.float32)
    shares = lax.psum_scatter(partial_out, "head", scatter_dimension=1, tiled=True)
    return (residual.astype(jnp.float32) + shares * wo_scales).astype(jnp.bfloat16)


def solution(mesh):
    placed = (
        P(("group", "dp"), "head"),
        P(("group", "dp"), None, None),
        P(("group", "dp")),
        P(("group", "dp")),
        P(("group", "dp"), None, "head", None),
        P(("group", "dp"), None, None, "head"),
        P("head", None),
        P("head"),
        P(("group", "dp"), "head"),
    )
    return jax.shard_map(
        on_device, mesh=mesh, in_specs=placed, out_specs=P(("group", "dp"), "head"), check_vma=False
    )
```

profile of v0, /device:TPU:0, one launch (start us, length us, event | category | flops | bytes accessed | tf_op | source)
XLA Modules:
  0.0 189.6 jit_solution(9036702720797545421)
XLA Ops:
  6.6 0.7 convert_element_type.50
  7.2 0.8 bitcast_convert_fusion
  8.0 0.8 slice_bitcast_fusion
  8.8 0.1 multiply_cosine_fusion
  8.9 0.1 multiply_subtract_fusion
  9.0 0.1 fusion.68
  9.1 32.6 %all_gather.3 = bf16[8,16384]{1,0:T(8,128)(2,1)S(1)} all-gather(bf16[8,2048]{1,0:T(8,128)(2,1)S(1)} %fusion.68), channel_id=1, replica_groups=mesh['group'=2,'head'=8,'dp'=2] {'head'}, dimensions={1}, use_global_device_ids=true | all-gather | bytes 294912 | tf_op jit(solution)/shard_map/all_gather | solution.py:78
  41.7 1.3 fusion.64
  43.0 0.1 copy.40
  43.1 0.7 broadcast_compare_fusion
  43.8 0.5 fusion.65
  44.3 0.4 fusion.6
  44.7 0.7 reshape.144
  45.4 5.5 %all-to-all-start.2 = ((f32[8,1,128]{2,1,0:T(1,128)}), f32[8,1,128]{2,1,0:T(1,128)S(1)}, u32[]{:S(2)}, u32[]{:S(2)}) async-start(f32[8,1,128]{2,1,0:T(1,128)} %reshape.144), calls=%async_computation.2 | async-start | bytes 8192 | tf_op jit(solution)/shard_map/all_to_all | solution.py:109
  50.9 0.9 slice_convert_fusion
  51.8 0.1 copy.41
  51.9 0.7 fusion.2
  52.6 0.1 add_convert_fusion.1
  52.7 0.7 reshape.142
  53.4 4.0 %all-to-all-done.2 = f32[8,1,128]{2,1,0:T(1,128)S(1)} async-done(((f32[8,1,128]{2,1,0:T(1,128)}), f32[8,1,128]{2,1,0:T(1,128)S(1)}, u32[]{:S(2)}, u32[]{:S(2)}) %all-to-all-start.2) | async-done | bytes 4128 | tf_op jit(solution)/shard_map/all_to_all | solution.py:109
  57.4 3.3 %all-to-all-start.1 = ((f32[8,1,128]{2,1,0:T(1,128)}), f32[8,1,128]{2,1,0:T(1,128)S(1)}, u32[]{:S(2)}, u32[]{:S(2)}) async-start(f32[8,1,128]{2,1,0:T(1,128)} %reshape.142), calls=%async_computation.1 | async-start | bytes 8192 | tf_op jit(solution)/shard_map/all_to_all | solution.py:108
  60.7 0.1 maximum_convert_fusion
  60.8 1.1 copy.29
  61.9 5.3 %all-to-all-done.1 = f32[8,1,128]{2,1,0:T(1,128)S(1)} async-done(((f32[8,1,128]{2,1,0:T(1,128)}), f32[8,1,128]{2,1,0:T(1,128)S(1)}, u32[]{:S(2)}, u32[]{:S(2)}) %all-to-all-start.1) | async-done | bytes 4128 | tf_op jit(solution)/shard_map/all_to_all | solution.py:108
  67.2 3.5 %all-to-all-start = ((f32[8,128,128]{2,0,1:T(8,128)}), f32[8,128,128]{2,0,1:T(8,128)S(1)}, u32[]{:S(2)}, u32[]{:S(2)}) async-start(f32[8,128,128]{2,0,1:T(8,128)} %copy.29), calls=%async_computation | async-start | bytes 1048576 | tf_op jit(solution)/shard_map/all_to_all | solution.py:110
  70.7 0.0 reduce-scatter.2.cloned.1.call-start
  70.7 0.2 fusion.15
  70.9 0.5 broadcast.103
  71.5 0.7 reduce.1
  72.1 0.1 reshape.143
  72.2 0.7 reduce.2
  72.9 0.1 reshape.145
  73.0 0.1 copy.34
  73.1 0.1 copy.32
  73.2 0.1 copy.31
  73.2 8.1 %all-to-all-done = f32[8,128,128]{2,0,1:T(8,128)S(1)} async-done(((f32[8,128,128]{2,0,1:T(8,128)}), f32[8,128,128]{2,0,1:T(8,128)S(1)}, u32[]{:S(2)}, u32[]{:S(2)}) %all-to-all-start) | async-done | bytes 524320 | tf_op jit(solution)/shard_map/all_to_all | solution.py:110
  81.3 0.2 multiply_reduce_fusion
  81.5 0.1 divide_convert_fusion
  81.6 0.2 convolution_bitcast_fusion
  81.8 0.1 collective-permute-start
  81.9 4.2 %collective-permute-done = f32[8,16,128]{2,1,0:T(8,128)S(1)} collective-permute-done((f32[8,16,128]{2,1,0:T(8,128)S(1)}, f32[8,16,128]{2,1,0:T(8,128)S(1)}, u32[]{:S(2)}, u32[]{:S(2)}) %collective-permute-start) | collective-permute-done | bytes 65568 | tf_op jit(solution)/shard_map/ppermute | solution.py:22
  86.1 0.4 collective-permute-start.1
  86.6 3.9 %collective-permute-done.1 = f32[8,16,128]{2,1,0:T(8,128)S(1)} collective-permute-done((f32[8,16,128]{2,1,0:T(8,128)S(1)}, f32[8,16,128]{2,1,0:T(8,128)S(1)}, u32[]{:S(2)}, u32[]{:S(2)}) %collective-permute-start.1) | collective-permute-done | bytes 65568 | tf_op jit(solution)/shard_map/ppermute | solution.py:22
  90.5 0.4 collective-permute-start.2
  90.9 5.3 %collective-permute-done.2 = f32[8,16,128]{2,1,0:T(8,128)S(1)} collective-permute-done((f32[8,16,128]{2,1,0:T(8,128)S(1)}, f32[8,16,128]{2,1,0:T(8,128)S(1)}, u32[]{:S(2)}, u32[]{:S(2)}) %collective-permute-start.2) | collective-permute-done | bytes 65568 | tf_op jit(solution)/shard_map/ppermute | solution.py:22
  96.2 23.4 %fusion.12 = f32[8,16384]{1,0:T(8,128)} fusion(bf16[2048,16384]{1,0:T(8,128)(2,1)} %param.15, bf16[1,8,16,128]{3,2,1,0:T(8,128)(2,1)S(1)} %fusion.11), kind=kOutput, calls=%fused_computation.24 | convolution fusion | flops 536870912 | bytes 67665920 | tf_op jit(solution)/shard_map/dot_general | solution.py:133
  119.7 61.6 %reduce-scatter.2.cloned.1.call-done = f32[8,2048]{1,0:T(8,128)} async-done(((f32[8,16384]{1,0:T(8,128)}), f32[8,2048]{1,0:T(8,128)}) %reduce-scatter.2.cloned.1.call-update) | async-done | bytes 65552 | tf_op jit(solution)/shard_map/reduce_scatter | solution.py:134
  181.3 1.5 add_convert_fusion
  (18 shorter events, 0.2 us)
Async XLA Ops:
  6.5 174.7 %copy-start = (bf16[8,2048]{1,0:T(8,128)(2,1)S(1)}, bf16[8,2048]{1,0:T(8,128)(2,1)}, u32[]{:S(2)}) copy-start(bf16[8,2048]{1,0:T(8,128)(2,1)} %param.17) | copy-start | bytes 98308
  6.5 174.7 %copy-start.1 = (f32[2048]{0:T(1024)S(1)}, f32[2048]{0:T(1024)}, u32[]{:S(2)}) copy-start(f32[2048]{0:T(1024)} %param.16) | copy-start | bytes 24580
  45.4 12.0 %all-to-all-start.2 = ((f32[8,1,128]{2,1,0:T(1,128)}), f32[8,1,128]{2,1,0:T(1,128)S(1)}, u32[]{:S(2)}, u32[]{:S(2)}) async-start(f32[8,1,128]{2,1,0:T(1,128)} %reshape.144), calls=%async_computation.2 | async-start | bytes 8192 | tf_op jit(solution)/shard_map/all_to_all | solution.py:109
  57.4 9.8 %all-to-all-start.1 = ((f32[8,1,128]{2,1,0:T(1,128)}), f32[8,1,128]{2,1,0:T(1,128)S(1)}, u32[]{:S(2)}, u32[]{:S(2)}) async-start(f32[8,1,128]{2,1,0:T(1,128)} %reshape.142), calls=%async_computation.1 | async-start | bytes 8192 | tf_op jit(solution)/shard_map/all_to_all | solution.py:108
  67.2 14.1 %all-to-all-start = ((f32[8,128,128]{2,0,1:T(8,128)}), f32[8,128,128]{2,0,1:T(8,128)S(1)}, u32[]{:S(2)}, u32[]{:S(2)}) async-start(f32[8,128,128]{2,0,1:T(8,128)} %copy.29), calls=%async_computation | async-start | bytes 1048576 | tf_op jit(solution)/shard_map/all_to_all | solution.py:110
  70.7 110.6 %reduce-scatter.2.cloned.1.call-start = ((), (), s32[]{:S(2)}) async-start(), calls=%async_computation.4 | async-start | bytes 589824 | tf_op jit(solution)/shard_map/reduce_scatter | solution.py:134
  81.8 4.3 %collective-permute-start = (f32[8,16,128]{2,1,0:T(8,128)S(1)}, f32[8,16,128]{2,1,0:T(8,128)S(1)}, u32[]{:S(2)}, u32[]{:S(2)}) collective-permute-start(f32[8,16,128]{2,1,0:T(8,128)S(1)} %convolution_bitcast_fusion), channel_id=1, source_target_pairs={{0,2},{2,0},{4,6},{6,4},{8,10},{10,8},{12,14},{14,12},{1,3},{3,1},... | collective-permute-start | bytes 196616 | tf_op jit(solution)/shard_map/ppermute | solution.py:22
  86.1 4.3 %collective-permute-start.1 = (f32[8,16,128]{2,1,0:T(8,128)S(1)}, f32[8,16,128]{2,1,0:T(8,128)S(1)}, u32[]{:S(2)}, u32[]{:S(2)}) collective-permute-start(f32[8,16,128]{2,1,0:T(8,128)S(1)} %add_select_fusion.1), channel_id=1, source_target_pairs={{0,4},{4,0},{2,6},{6,2},{8,12},{12,8},{10,14},{14,10},{1,5},{5,1},... | collective-permute-start | bytes 196616 | tf_op jit(solution)/shard_map/ppermute | solution.py:22
  90.5 5.7 %collective-permute-start.2 = (f32[8,16,128]{2,1,0:T(8,128)S(1)}, f32[8,16,128]{2,1,0:T(8,128)S(1)}, u32[]{:S(2)}, u32[]{:S(2)}) collective-permute-start(f32[8,16,128]{2,1,0:T(8,128)S(1)} %add_select_fusion), channel_id=1, source_target_pairs={{0,8},{8,0},{2,10},{10,2},{4,12},{12,4},{6,14},{14,6},{1,9},{9,1},... | collective-permute-start | bytes 196616 | tf_op jit(solution)/shard_map/ppermute | solution.py:22
Sparse Core Ops, SparseCore 0:
  119.8 61.4 reduce-scatter.1
where the time goes:
time: 190 us
  waiting for transfers between devices  92.4 us (49%)
  blocking collectives  32.6 us (17%)
  matrix products  24.9 us (13%)
  between operations  13.6 us (7%)
  starting transfers between devices  13.3 us (7%)
  other arithmetic  7.09 us (4%)
  local copies, waits for them, and re-layouts  5.66 us (3%)
    reduce_scatter x1, waiting for transfers between devices, on_device(): lax.psum_scatter(partial_out, 'head', scatter_dimension=1, tiled=True)  61.6 us
    all_gather x1, blocking collectives, on_device(): lax.all_gather(own_query.reshape(n_rows, heads_here * HD), 'head', axis=1...  32.6 us
    dot_general x1, matrix products, on_device(): jnp.dot(flat_rows, wo_codes, preferred_element_type=jnp.float32)  23.4 us
    ppermute x3, waiting for transfers between devices, partner_2(): return lax.ppermute(block, axis, route)  13.4 us
    all_to_all x1, waiting for transfers between devices, on_device(): lax.all_to_all(summed_full, 'head', split_axis=1, concat_axis=1, tiled=True)  8.07 us
    all_to_all x1, starting transfers between devices, on_device(): lax.all_to_all(total_full, 'head', split_axis=1, concat_axis=1, tiled=True)  5.52 us
    all_to_all x1, waiting for transfers between devices, on_device(): lax.all_to_all(peak_full, 'head', split_axis=1, concat_axis=1, tiled=True)  5.27 us
    all_to_all x1, waiting for transfers between devices, on_device(): lax.all_to_all(total_full, 'head', split_axis=1, concat_axis=1, tiled=True)  4.03 us
  transfers between devices with their start and end apart: 7, of which 7 were waited for; matrix products, arithmetic and copies ran while one was open for 3% of the time, Pallas kernels for 0%

commit v1 on v0

v1 whole, which is shorter than its diff:
```python
import functools
import jax
import jax.numpy as jnp
from jax import lax
from jax.experimental import pallas as pl
from jax.experimental.pallas import tpu as pltpu
from jax.sharding import PartitionSpec as P

HD = 128
ROPE_BASE = 500000.0
NEG_FILL = -1e30
STAT_ROWS = 16
MIB = 1 << 20
VMEM = pltpu.MemorySpace.VMEM
SMEM = pltpu.MemorySpace.SMEM


def split3(value):
    high = value.astype(jnp.bfloat16)
    rest = value - high.astype(jnp.float32)
    middle = rest.astype(jnp.bfloat16)
    low = (rest - middle.astype(jnp.float32)).astype(jnp.bfloat16)
    return high, middle, low


def contract(left, right, dims):
    return lax.dot_general(left, right, (dims, ((), ())), preferred_element_type=jnp.float32)


def rotary_tables(positions):
    half_dim = HD // 2
    inverse_rate = ROPE_BASE ** (-(jnp.arange(half_dim, dtype=jnp.float32) * (2.0 / HD)))
    angles = positions.astype(jnp.float32)[:, None] * inverse_rate
    cosine = jnp.cos(angles)
    sine = jnp.sin(angles)
    return jnp.concatenate([cosine, cosine], -1), jnp.concatenate([-sine, sine], -1)


def attend(scalars, gathered, cosine, sine, new_kv, kv_codes, key_scales, value_scales):
    n_src, n_rows, width = gathered.shape
    heads_here = width // HD
    n_heads = n_src * heads_here
    block_len = kv_codes.shape[2]
    n_kv = kv_codes.shape[3] // HD
    group = n_heads // n_kv
    score_scale = HD ** (-0.5)

    def body(s_ref, q_ref, cos_ref, sin_ref, new_ref, kv_ref, ks_ref, vs_ref, out_ref, qs, ks):
        cos, sin = cos_ref[...], sin_ref[...]

        def rotate(tile):
            return tile * cos + pltpu.roll(tile, HD // 2, 1) * sin

        for src in range(n_src):
            block = q_ref[src].astype(jnp.float32)
            for j in range(heads_here):
                head = src * heads_here + j
                qs[n_rows * head : n_rows * (head + 1), :] = rotate(block[:, HD * j : HD * (j + 1)])
        fresh = new_ref[:, 0, :].astype(jnp.float32)
        for k in range(n_kv):
            ks[n_rows * k : n_rows * (k + 1), :] = rotate(fresh[:, HD * k : HD * (k + 1)])

        first_slot = s_ref[n_rows]
        is_first = first_slot == 0
        lane_group = lax.broadcasted_iota(jnp.int32, (1, n_heads), 1) // group
        slot = first_slot + lax.broadcasted_iota(jnp.int32, (block_len, n_heads), 0)
        own_kv = lax.broadcasted_iota(jnp.int32, (n_kv, n_heads), 0) == lane_group
        for r in range(n_rows):
            query = qs[pl.ds(r, n_heads, stride=n_rows), :].astype(jnp.bfloat16)
            keys = jnp.concatenate(
                [kv_ref[r, 0, :, HD * k : HD * (k + 1)] for k in range(n_kv)], axis=0
            )
            values = jnp.concatenate(
                [kv_ref[r, 1, :, HD * k : HD * (k + 1)] for k in range(n_kv)], axis=0
            )
            raw = contract(keys, query, ((1,), (1,)))
            raw_own = jnp.zeros((block_len, n_heads), jnp.float32)
            for k in range(n_kv):
                raw_own = jnp.where(lane_group == k, raw[block_len * k : block_len * (k + 1)], raw_own)
            is_valid = slot < s_ref[r]
            scores = jnp.where(is_valid, raw_own * ks_ref[r] * score_scale, NEG_FILL)
            fresh_key = ks[pl.ds(r, n_kv, stride=n_rows), :].astype(jnp.bfloat16)
            fresh_raw = contract(fresh_key, query, ((1,), (1,)))
            fresh_score = jnp.sum(jnp.where(own_kv, fresh_raw, 0.0), axis=0, keepdims=True) * score_scale
            fresh_score = jnp.where(is_first, fresh_score, NEG_FILL)
            peak = jnp.maximum(jnp.max(scores, axis=0, keepdims=True), fresh_score)
            weights = jnp.where(is_valid, jnp.exp(scores - peak), 0.0)
            fresh_weight = jnp.where(is_first, jnp.exp(fresh_score - peak), 0.0)
            total = jnp.sum(weights, axis=0, keepdims=True) + fresh_weight
            scaled = weights * vs_ref[r]
            spread = jnp.concatenate(
                [jnp.where(lane_group == k, scaled, 0.0) for k in range(n_kv)], axis=0
            )
            high = spread.astype(jnp.bfloat16)
            low = (spread - high.astype(jnp.float32)).astype(jnp.bfloat16)
            fresh_spread = jnp.where(own_kv, fresh_weight, 0.0)
            fresh_high = fresh_spread.astype(jnp.bfloat16)
            fresh_low = (fresh_spread - fresh_high.astype(jnp.float32)).astype(jnp.bfloat16)
            fresh_value = jnp.concatenate(
                [new_ref[r : r + 1, 1, HD * k : HD * (k + 1)] for k in range(n_kv)], axis=0
            )
            both = ((0,), (0,))
            summed = contract(high, values, both) + contract(low, values, both)
            summed = summed + (
                contract(fresh_high, fresh_value, both) + contract(fresh_low, fresh_value, both)
            )
            out_ref[r, 0:n_heads, :] = summed.astype(jnp.bfloat16)
            parts = split3(peak) + split3(total)
            pad = jnp.zeros((STAT_ROWS - len(parts), n_heads), jnp.float32)
            stats = jnp.concatenate([part.astype(jnp.float32) for part in parts] + [pad], axis=0)
            out_ref[r, n_heads : n_heads + STAT_ROWS, :] = stats.astype(jnp.bfloat16)

    return pl.pallas_call(
        body,
        out_shape=jax.ShapeDtypeStruct((n_rows, n_heads + STAT_ROWS, HD), jnp.bfloat16),
        in_specs=[pl.BlockSpec(memory_space=SMEM)] + [pl.BlockSpec(memory_space=VMEM)] * 7,
        out_specs=pl.BlockSpec(memory_space=VMEM),
        scratch_shapes=[
            pltpu.VMEM((n_rows * n_heads, HD), jnp.float32),
            pltpu.VMEM((n_rows * n_kv, HD), jnp.float32),
        ],
        compiler_params=pltpu.CompilerParams(vmem_limit_bytes=12 * MIB),
        name="attend",
    )(scalars, gathered, cosine, sine, new_kv, kv_codes, key_scales, value_scales)


def settle(main, stats, n_heads, stat_row):
    n_src = main.shape[0]
    depth = main.shape[2]
    heads_root = n_heads ** (-0.5)

    def body(main_ref, stat_ref, out_ref):
        peaks, totals = [], []
        for b in range(n_src):
            part = stat_ref[b, stat_row : stat_row + STAT_ROWS, :].astype(jnp.float32)
            peaks.append(part[0:1] + part[1:2] + part[2:3])
            totals.append(part[3:4] + part[4:5] + part[5:6])
        peak = functools.reduce(jnp.maximum, peaks)
        scales = [jnp.exp(p - peak) for p in peaks]
        total = functools.reduce(jnp.add, [s * t for s, t in zip(scales, totals)])
        common = lax.broadcasted_iota(jnp.int32, (n_heads, n_heads), 0) & lax.broadcasted_iota(
            jnp.int32, (n_heads, n_heads), 1
        )
        bits = (n_heads - 1).bit_length()
        parity = common
        for bit in range(1, bits):
            parity = parity ^ (common >> bit)
        sign = jnp.where((parity & 1) == 0, heads_root, -heads_root)
        acc = jnp.zeros((n_heads, depth), jnp.float32)
        for b in range(n_src):
            mixed = sign * (scales[b] / total)
            high = mixed.astype(jnp.bfloat16)
            low = (mixed - high.astype(jnp.float32)).astype(jnp.bfloat16)
            value = main_ref[b, 0:n_heads, :]
            acc = acc + jnp.dot(high, value, preferred_element_type=jnp.float32)
            acc = acc + jnp.dot(low, value, preferred_element_type=jnp.float32)
        out_ref[...] = acc.astype(jnp.bfloat16)

    return pl.pallas_call(
        body,
        out_shape=jax.ShapeDtypeStruct((n_heads, depth), jnp.bfloat16),
        in_specs=[pl.BlockSpec(memory_space=VMEM)] * 2,
        out_specs=pl.BlockSpec(memory_space=VMEM),
        compiler_params=pltpu.CompilerParams(vmem_limit_bytes=16 * MIB),
        name="settle",
    )(main, stats)


def project(own_share, rows, wo, n_block, n_share):
    n_all, heads_here, _ = rows.shape
    depth = wo.shape[0]
    block_cols = wo.shape[1] // n_block
    piece = block_cols // n_share
    n_rows = n_all // n_share

    def body(own_ref, x_ref, wo_ref, out_ref, weights, wide, packed, sem):
        start = own_ref[0] * piece

        def fetch(b):
            cols = pl.ds(pl.multiple_of(b * block_cols + start, 128), piece)
            return pltpu.make_async_copy(wo_ref.at[:, cols], weights.at[b], sem.at[b])

        for b in range(n_block):
            fetch(b).start()
        wide[...] = x_ref[...].astype(jnp.float32).reshape(n_all * heads_here, HD)
        for j in range(heads_here):
            pieces = [
                wide[pl.ds(s * heads_here + j, n_rows, stride=heads_here * n_share), :]
                for s in range(n_share)
            ]
            packed[:, HD * j : HD * (j + 1)] = jnp.concatenate(pieces, axis=0).astype(jnp.bfloat16)
        x = packed[...]
        for b in range(n_block):
            fetch(b).wait()
            share = jnp.dot(x, weights[b], preferred_element_type=jnp.float32)
            for s in range(n_share):
                out_ref[b * n_share + s] = share[s * n_rows : (s + 1) * n_rows].astype(jnp.bfloat16)

    return pl.pallas_call(
        body,
        out_shape=jax.ShapeDtypeStruct((n_block * n_share, n_rows, piece), jnp.bfloat16),
        in_specs=[
            pl.BlockSpec(memory_space=SMEM),
            pl.BlockSpec(memory_space=VMEM),
            pl.BlockSpec(memory_space=pl.ANY),
        ],
        out_specs=pl.BlockSpec(memory_space=VMEM),
        scratch_shapes=[
            pltpu.VMEM((n_block, depth, piece), wo.dtype),
            pltpu.VMEM((n_all * heads_here, HD), jnp.float32),
            pltpu.VMEM((n_all, heads_here * HD), jnp.bfloat16),
            pltpu.SemaphoreType.DMA((n_block,)),
        ],
        compiler_params=pltpu.CompilerParams(vmem_limit_bytes=44 * MIB),
        name="project",
    )(own_share, rows, wo)


def finish(shares, scales, residual, n_share):
    n_all, n_rows, piece = shares.shape

    def body(share_ref, scale_ref, res_ref, out_ref):
        for s in range(n_share):
            total = share_ref[s].astype(jnp.float32)
            for h in range(1, n_all // n_share):
                total = total + share_ref[h * n_share + s].astype(jnp.float32)
            cols = slice(s * piece, (s + 1) * piece)
            out_ref[:, cols] = (
                res_ref[:, cols].astype(jnp.float32) + total * scale_ref[:, cols]
            ).astype(jnp.bfloat16)

    return pl.pallas_call(
        body,
        out_shape=jax.ShapeDtypeStruct(residual.shape, jnp.bfloat16),
        in_specs=[pl.BlockSpec(memory_space=VMEM)] * 3,
        out_specs=pl.BlockSpec(memory_space=VMEM),
        compiler_params=pltpu.CompilerParams(vmem_limit_bytes=16 * MIB),
        name="finish",
    )(shares, scales, residual)


def exchange(block, axes):
    return lax.all_to_all(block, axes, split_axis=0, concat_axis=0, tiled=True)


def on_device(
    queries, new_kv, positions, lengths, kv_codes, kv_scales, wo_codes, wo_scales, residual
):
    n_head = lax.axis_size("head")
    n_share = lax.axis_size("dp")
    my_head = lax.axis_index("head")
    my_share = lax.axis_index("dp")
    n_rows, width = queries.shape
    heads_here = width // HD
    n_heads = heads_here * n_head
    n_kv = new_kv.shape[2] // HD
    block_len = kv_codes.shape[2]
    own_cols = wo_codes.shape[1] // n_head

    gathered = exchange(jnp.broadcast_to(queries, (n_head, n_rows, width)), "head")
    cosine, sine = rotary_tables(positions)
    spread = jnp.repeat(jnp.swapaxes(kv_scales, 2, 3), n_heads // n_kv, axis=3)
    scalars = jnp.concatenate([lengths, (my_head * block_len).reshape(1)]).astype(jnp.int32)
    partial = attend(
        scalars, gathered, cosine, sine, new_kv, kv_codes, spread[:, 0], spread[:, 1]
    )

    cuts = max(1, n_head // n_rows)
    depth = HD // cuts
    if cuts == 1:
        main = exchange(partial, "head")
        rotated = settle(main, main, n_heads, n_heads)
    else:
        values = partial[:, :n_heads].reshape(n_rows, n_heads, cuts, depth).swapaxes(1, 2)
        stats = partial[:, n_heads:].reshape(n_rows, 1, STAT_ROWS * cuts, depth)
        stats = jnp.broadcast_to(stats, (n_rows, cuts) + stats.shape[2:])
        message = jnp.concatenate([values, stats], axis=2)
        received = exchange(message.reshape((n_head,) + message.shape[2:]), "head")
        rotated = settle(
            received[:, :n_heads], received[:, n_heads:].reshape(n_head, STAT_ROWS, HD), n_heads, 0
        )
    copies = jnp.broadcast_to(
        rotated.reshape(n_head, 1, heads_here, depth), (n_head, n_share, heads_here, depth)
    )
    rows = exchange(copies.reshape(n_head * n_share, heads_here, depth), ("head", "dp"))
    if cuts > 1:
        rows = rows.reshape(n_rows, cuts, n_share, heads_here, depth).transpose(0, 2, 3, 1, 4)
        rows = rows.reshape(n_rows * n_share, heads_here, HD)
    shares = exchange(
        project(my_share.reshape(1).astype(jnp.int32), rows, wo_codes, n_head, n_share), ("head", "dp"))
    return finish(shares, wo_scales.reshape(1, own_cols), residual, n_share)


def solution(mesh):
    placed = (
        P(("group", "dp"), "head"),
        P(("group", "dp"), None, None),
        P(("group", "dp")),
        P(("group", "dp")),
        P(("group", "dp"), None, "head", None),
        P(("group", "dp"), None, None, "head"),
        P("head", None),
        P("head"),
        P(("group", "dp"), "head"),
    )
    return jax.shard_map(
        on_device, mesh=mesh, in_specs=placed, out_specs=P(("group", "dp"), "head"), check_vma=False
    )
```

time: 190 us -> 73 us (0.38)
  waiting for transfers between devices: 92.4 us -> 12.8 us
  matrix products: 24.9 us -> 0 us
  Pallas kernels: 0 us -> 15.6 us
  between operations: 13.6 us -> 0.07 us
  blocking collectives: 32.6 us -> 26 us
  other arithmetic: 7.09 us -> 1.59 us
  starting transfers between devices: 13.3 us -> 10.8 us
    reduce_scatter x1 -> x0, waiting for transfers between devices: 61.6 us -> none  [on_device(): lax.psum_scatter(partial_out, 'head', scatter_dimension=1, tiled=True)]
    all_gather x1 -> x0, blocking collectives: 32.6 us -> none  [on_device(): lax.all_gather(own_query.reshape(n_rows, heads_here * HD), 'head', axis=1...]
    all_to_all x0 -> x2, blocking collectives: none -> 26 us  [exchange(): return lax.all_to_all(block, axes, split_axis=0, concat_axis=0, tiled=True)]
    dot_general x5 -> x0, matrix products: 24.9 us -> none  [the longest x1 23.4 us: on_device(): jnp.dot(flat_rows, wo_codes, preferred_element_type=jnp.float32)]
    pallas_call x0 -> x4, Pallas kernels: none -> 15.6 us  [the longest x1 11.5 us: project(): pl.pallas_call(body, out_shape=jax.ShapeDtypeStruct((n_block * n_share, n...]
    ppermute x3 -> x0, waiting for transfers between devices: 13.4 us -> none  [partner_2(): return lax.ppermute(block, axis, route)]
    all_to_all x3 -> x2, waiting for transfers between devices: 17.4 us -> 12.8 us  [exchange(): return lax.all_to_all(block, axes, split_axis=0, concat_axis=0, tiled=True)]
    convert_element_type x7 -> x1, other arithmetic: 4.05 us -> 0.66 us  [rotary_tables(): angles = positions.astype(jnp.float32)[:, None] * inverse_rate]
  transfers between devices with their start and end apart: 7 -> 2, of which waited for: 7 -> 2; matrix products, arithmetic and copies ran while one was open for 3% -> 4% of each run, Pallas kernels for 0% -> 0%
where the time goes in v1:
time: 73 us; the launch traced here: 72.4 us
  blocking collectives  26 us (36%)
  Pallas kernels  15.6 us (21%)
  waiting for transfers between devices  12.8 us (18%)
  starting transfers between devices  10.8 us (15%)
  local copies, waits for them, and re-layouts  5.47 us (7%)
  other arithmetic  1.59 us (2%)
    all_to_all x2, blocking collectives, exchange(): return lax.all_to_all(block, axes, split_axis=0, concat_axis=0, tiled=True)  26 us
    all_to_all x2, waiting for transfers between devices, exchange(): return lax.all_to_all(block, axes, split_axis=0, concat_axis=0, tiled=True)  12.8 us
    pallas_call x1, Pallas kernels, project(): pl.pallas_call(body, out_shape=jax.ShapeDtypeStruct((n_block * n_share, n...  11.5 us
    all_to_all x2, starting transfers between devices, exchange(): return lax.all_to_all(block, axes, split_axis=0, concat_axis=0, tiled=True)  10.8 us
    pallas_call x1, Pallas kernels, attend(): pl.pallas_call(body, out_shape=jax.ShapeDtypeStruct((n_rows, n_heads + ST...  3.14 us
    unnamed x10, local copies, waits for them, and re-layouts  2.33 us
    broadcast_in_dim x1, local copies, waits for them, and re-layouts, on_device(): jnp.broadcast_to(queries, (n_head, n_rows, width))  1.5 us
  transfers between devices with their start and end apart: 2, of which 2 were waited for; matrix products, arithmetic and copies ran while one was open for 4% of the time, Pallas kernels for 0%

profile of v1, /device:TPU:0, one launch (start us, length us, event | category | flops | bytes accessed | tf_op | source)
XLA Modules:
  0.0 72.4 jit_solution(13730108730017536836)
XLA Ops:
  0.0 0.0 copy-start.3
  0.0 0.0 copy-start.2
  0.0 1.5 %broadcast_in_dim.15 = bf16[8,8,2048]{2,1,0:T(8,128)(2,1)} broadcast(bf16[8,2048]{1,0:T(8,128)(2,1)} %param.9), dimensions={1,2} | broadcast | bytes 294912 | tf_op jit(solution)/shard_map/broadcast_in_dim | solution.py:260
  1.5 7.3 %all-to-all-start = ((bf16[8,8,2048]{2,1,0:T(8,128)(2,1)}), bf16[8,8,2048]{2,1,0:T(8,128)(2,1)S(1)}, u32[]{:S(2)}, u32[]{:S(2)}) async-start(bf16[8,8,2048]{2,1,0:T(8,128)(2,1)} %broadcast_in_dim.15), calls=%async_computation | async-start | bytes 524288 | tf_op jit(solution)/shard_map/all_to_all | solution.py:243
  8.8 0.9 %broadcast_in_dim.16 = f32[8,2,32,8,16]{2,4,3,1,0:T(8,128)S(1)} broadcast(f32[8,2,32,8]{2,3,1,0:T(8,128)} %bitcast.14), dimensions={0,1,2,3} | broadcast | bytes 278528 | tf_op jit(solution)/shard_map/broadcast_in_dim | solution.py:262
  9.7 0.1 fusion.1
  9.8 0.7 convert_element_type.3
  10.5 0.2 copy.13
  10.7 0.2 copy.14
  10.8 0.7 %pad_add_fusion.s_ref = s32[9]{0:T(128)S(1)} fusion(s32[1]{0:T(128)} %bitcast.1, s32[8]{0:T(128)} %param.12), kind=kLoop, calls=%fused_computation.5 | loop fusion | flops 9 | bytes 72 | tf_op jit(solution)/shard_map/concatenate | solution.py:263
  11.6 0.1 fusion
  11.7 0.1 pad_maximum_fusion
  11.8 6.0 %all-to-all-done.q_ref = bf16[8,8,2048]{2,1,0:T(8,128)(2,1)S(1)} async-done(((bf16[8,8,2048]{2,1,0:T(8,128)(2,1)}), bf16[8,8,2048]{2,1,0:T(8,128)(2,1)S(1)}, u32[]{:S(2)}, u32[]{:S(2)}) %all-to-all-start) | async-done | bytes 262176 | tf_op jit(solution)/shard_map/all_to_all | solution.py:243
  17.7 0.0 copy-start
  17.7 1.2 %copy-done = bf16[8,2,32,1024]{3,2,1,0:T(8,128)(2,1)S(1)} copy-done((bf16[8,2,32,1024]{3,2,1,0:T(8,128)(2,1)S(1)}, bf16[8,2,32,1024]{3,2,1,0:T(8,128)(2,1)}, u32[]{:S(2)}) %copy-start) | copy-done | bytes 1048600
  18.9 0.0 copy-start.1
  18.9 0.8 %copy-done.1 = bf16[8,2,1024]{2,1,0:T(2,128)(2,1)S(1)} copy-done((bf16[8,2,1024]{2,1,0:T(2,128)(2,1)S(1)}, bf16[8,2,1024]{2,1,0:T(2,128)(2,1)}, u32[]{:S(2)}) %copy-start.1) | copy-done | bytes 32792
  19.7 3.1 %attend.1 = bf16[8,144,128]{2,1,0:T(8,128)(2,1)S(1)} custom-call(s32[9]{0:T(128)S(1)} %pad_add_fusion.s_ref, bf16[8,8,2048]{2,1,0:T(8,128)(2,1)S(1)} %all-to-all-done.q_ref, f32[8,128]{1,0:T(8,128)S(1)} %get-tuple-element.10.cos_ref, f32[8,128]{1,0:T(8,128)S(1)} %get-tuple-element.11.sin_ref, bf16[8,2,1024]{2,1,0:T(2,128)(2,1)S(1)} %copy-done.1, ...), custom_call_target="tpu_custom_call" | custom-call | tf_op jit(solution)/shard_map/attend/pallas_call | solution.py:113
  22.8 13.4 %all_to_all.20.main_ref.stat_ref = bf16[8,144,128]{2,1,0:T(8,128)(2,1)S(1)} all-to-all(bf16[8,144,128]{2,1,0:T(8,128)(2,1)S(1)} %attend.1), channel_id=1, replica_groups=mesh['group'=2,'head'=8,'dp'=2] {'head'}, dimensions={0} | all-to-all | bytes 589824 | tf_op jit(solution)/shard_map/all_to_all | solution.py:243
  36.3 0.3 settle.1
  36.6 0.6 broadcast_in_dim.18
  37.2 3.5 %all-to-all-start.2 = ((bf16[16,16,128]{2,1,0:T(8,128)(2,1)}), bf16[16,16,128]{2,1,0:T(8,128)(2,1)S(1)}, u32[]{:S(2)}, u32[]{:S(2)}) async-start(bf16[16,16,128]{2,1,0:T(8,128)(2,1)} %bitcast.7), calls=%async_computation.2 | async-start | bytes 131072 | tf_op jit(solution)/shard_map/all_to_all | solution.py:243
  40.7 6.9 %all-to-all-done.2.x_ref = bf16[16,16,128]{2,1,0:T(8,128)(2,1)S(1)} async-done(((bf16[16,16,128]{2,1,0:T(8,128)(2,1)}), bf16[16,16,128]{2,1,0:T(8,128)(2,1)S(1)}, u32[]{:S(2)}, u32[]{:S(2)}) %all-to-all-start.2) | async-done | bytes 65568 | tf_op jit(solution)/shard_map/all_to_all | solution.py:243
  47.6 11.5 %project.1 = bf16[16,8,1024]{2,1,0:T(8,128)(2,1)S(1)} custom-call(s32[1]{0:T(128)} %bitcast.own_ref, bf16[16,16,128]{2,1,0:T(8,128)(2,1)S(1)} %all-to-all-done.2.x_ref, bf16[2048,16384]{1,0:T(8,128)(2,1)} %wo_ref.1), custom_call_target="tpu_custom_call" | custom-call | tf_op jit(solution)/shard_map/project/pallas_call | solution.py:199
  59.1 12.6 %all_to_all.21.share_ref = bf16[16,8,1024]{2,1,0:T(8,128)(2,1)S(1)} all-to-all(bf16[16,8,1024]{2,1,0:T(8,128)(2,1)S(1)} %project.1), channel_id=1, replica_groups=mesh['group'=2,'head'=8,'dp'=2] {'head','dp'}, dimensions={0} | all-to-all | bytes 524288 | tf_op jit(solution)/shard_map/all_to_all | solution.py:243
  71.7 0.0 copy-done.3
  71.7 0.0 copy-done.2
  71.7 0.7 finish.1
  (1 shorter events, 0.0 us)
Async XLA Ops:
  0.0 71.7 %copy-start.3 = (f32[2048]{0:T(1024)S(1)}, f32[2048]{0:T(1024)}, u32[]{:S(2)}) copy-start(f32[2048]{0:T(1024)} %param.16) | copy-start | bytes 24580
  0.0 71.7 %copy-start.2 = (bf16[8,2048]{1,0:T(8,128)(2,1)S(1)}, bf16[8,2048]{1,0:T(8,128)(2,1)}, u32[]{:S(2)}) copy-start(bf16[8,2048]{1,0:T(8,128)(2,1)} %res_ref.1) | copy-start | bytes 98308
  1.5 16.2 %all-to-all-start = ((bf16[8,8,2048]{2,1,0:T(8,128)(2,1)}), bf16[8,8,2048]{2,1,0:T(8,128)(2,1)S(1)}, u32[]{:S(2)}, u32[]{:S(2)}) async-start(bf16[8,8,2048]{2,1,0:T(8,128)(2,1)} %broadcast_in_dim.15), calls=%async_computation | async-start | bytes 524288 | tf_op jit(solution)/shard_map/all_to_all | solution.py:243
  17.7 1.2 %copy-start = (bf16[8,2,32,1024]{3,2,1,0:T(8,128)(2,1)S(1)}, bf16[8,2,32,1024]{3,2,1,0:T(8,128)(2,1)}, u32[]{:S(2)}) copy-start(bf16[8,2,32,1024]{3,2,1,0:T(8,128)(2,1)} %kv_ref.1) | copy-start | bytes 3145732
  18.9 0.8 %copy-start.1 = (bf16[8,2,1024]{2,1,0:T(2,128)(2,1)S(1)}, bf16[8,2,1024]{2,1,0:T(2,128)(2,1)}, u32[]{:S(2)}) copy-start(bf16[8,2,1024]{2,1,0:T(2,128)(2,1)} %new_ref.1) | copy-start | bytes 98308
  37.2 10.4 %all-to-all-start.2 = ((bf16[16,16,128]{2,1,0:T(8,128)(2,1)}), bf16[16,16,128]{2,1,0:T(8,128)(2,1)S(1)}, u32[]{:S(2)}, u32[]{:S(2)}) async-start(bf16[16,16,128]{2,1,0:T(8,128)(2,1)} %bitcast.7), calls=%async_computation.2 | async-start | bytes 131072 | tf_op jit(solution)/shard_map/all_to_all | solution.py:243

commit v2 on v1

--- a/solution.py
+++ b/solution.py
@@ -9,10 +9,11 @@
 HD = 128
 ROPE_BASE = 500000.0
 NEG_FILL = -1e30
-STAT_ROWS = 16
+STAT_ROWS = 8
 MIB = 1 << 20
 VMEM = pltpu.MemorySpace.VMEM
 SMEM = pltpu.MemorySpace.SMEM
+HBM = pltpu.MemorySpace.HBM
 
 
 def split3(value):
@@ -36,7 +37,18 @@
     return jnp.concatenate([cosine, cosine], -1), jnp.concatenate([-sine, sine], -1)
 
 
-def attend(scalars, gathered, cosine, sine, new_kv, kv_codes, key_scales, value_scales):
+def weight_fetch(wo_ref, out_ref, sem, share, n_block, piece):
+    def fetch(block, slot):
+        start = block * (wo_ref.shape[1] // n_block) + share * piece
+        cols = pl.ds(pl.multiple_of(start, 128), piece)
+        return pltpu.make_async_copy(wo_ref.at[:, cols], out_ref.at[slot], sem.at[slot])
+
+    return fetch
+
+
+def attend(
+    scalars, gathered, cosine, sine, new_kv, kv_codes, key_scales, value_scales, wo, n_early, piece
+):
     n_src, n_rows, width = gathered.shape
     heads_here = width // HD
     n_heads = n_src * heads_here
@@ -45,7 +57,21 @@
     group = n_heads // n_kv
     score_scale = HD ** (-0.5)
 
-    def body(s_ref, q_ref, cos_ref, sin_ref, new_ref, kv_ref, ks_ref, vs_ref, out_ref, qs, ks):
+    def body(
+        s_ref, q_ref, cos_ref, sin_ref, new_hbm, kv_hbm, ks_ref, vs_ref, wo_ref, out_ref, early_ref,
+        qs, ks, new_ref, kv_ref, new_sem, kv_sem, wo_sem,
+    ):
+        fetch_new = pltpu.make_async_copy(new_hbm, new_ref, new_sem)
+        fetch_new.start()
+        fetch_kv = [
+            pltpu.make_async_copy(kv_hbm.at[r], kv_ref.at[r], kv_sem.at[r]) for r in range(n_rows)
+        ]
+        for copy in fetch_kv:
+            copy.start()
+        fetch = weight_fetch(wo_ref, early_ref, wo_sem, s_ref[n_rows + 1], n_src, piece)
+        fetch_wo = [fetch(b, b) for b in range(n_early)]
+        for copy in fetch_wo:
+            copy.start()
         cos, sin = cos_ref[...], sin_ref[...]
 
         def rotate(tile):
@@ -56,6 +82,7 @@
             for j in range(heads_here):
                 head = src * heads_here + j
                 qs[n_rows * head : n_rows * (head + 1), :] = rotate(block[:, HD * j : HD * (j + 1)])
+        fetch_new.wait()
         fresh = new_ref[:, 0, :].astype(jnp.float32)
         for k in range(n_kv):
             ks[n_rows * k : n_rows * (k + 1), :] = rotate(fresh[:, HD * k : HD * (k + 1)])
@@ -66,6 +93,7 @@
         slot = first_slot + lax.broadcasted_iota(jnp.int32, (block_len, n_heads), 0)
         own_kv = lax.broadcasted_iota(jnp.int32, (n_kv, n_heads), 0) == lane_group
         for r in range(n_rows):
+            fetch_kv[r].wait()
             query = qs[pl.ds(r, n_heads, stride=n_rows), :].astype(jnp.bfloat16)
             keys = jnp.concatenate(
                 [kv_ref[r, 0, :, HD * k : HD * (k + 1)] for k in range(n_kv)], axis=0
@@ -109,25 +137,39 @@
             pad = jnp.zeros((STAT_ROWS - len(parts), n_heads), jnp.float32)
             stats = jnp.concatenate([part.astype(jnp.float32) for part in parts] + [pad], axis=0)
             out_ref[r, n_heads : n_heads + STAT_ROWS, :] = stats.astype(jnp.bfloat16)
-
+        for copy in fetch_wo:
+            copy.wait()
+
+    in_vmem, in_hbm = pl.BlockSpec(memory_space=VMEM), pl.BlockSpec(memory_space=HBM)
     return pl.pallas_call(
         body,
-        out_shape=jax.ShapeDtypeStruct((n_rows, n_heads + STAT_ROWS, HD), jnp.bfloat16),
-        in_specs=[pl.BlockSpec(memory_space=SMEM)] + [pl.BlockSpec(memory_space=VMEM)] * 7,
-        out_specs=pl.BlockSpec(memory_space=VMEM),
+        out_shape=(
+            jax.ShapeDtypeStruct((n_rows, n_heads + STAT_ROWS, HD), jnp.bfloat16),
+            pltpu.VMEM((n_early, wo.shape[0], piece), wo.dtype),
+        ),
+        in_specs=[pl.BlockSpec(memory_space=SMEM)]
+        + [in_vmem] * 3 + [in_hbm] * 2 + [in_vmem] * 2 + [in_hbm],
+        out_specs=(in_vmem, in_vmem),
         scratch_shapes=[
             pltpu.VMEM((n_rows * n_heads, HD), jnp.float32),
             pltpu.VMEM((n_rows * n_kv, HD), jnp.float32),
+            pltpu.VMEM(new_kv.shape, new_kv.dtype),
+            pltpu.VMEM(kv_codes.shape, kv_codes.dtype),
+            pltpu.SemaphoreType.DMA,
+            pltpu.SemaphoreType.DMA((n_rows,)),
+            pltpu.SemaphoreType.DMA((n_early,)),
         ],
         compiler_params=pltpu.CompilerParams(vmem_limit_bytes=12 * MIB),
         name="attend",
-    )(scalars, gathered, cosine, sine, new_kv, kv_codes, key_scales, value_scales)
-
-
-def settle(main, stats, n_heads, stat_row):
+    )(scalars, gathered, cosine, sine, new_kv, kv_codes, key_scales, value_scales, wo)
+
+
+def settle(main, stats, n_heads, stat_row, n_target, copies):
     n_src = main.shape[0]
     depth = main.shape[2]
     heads_root = n_heads ** (-0.5)
+    heads_out = n_heads // n_target
+    n_out = n_target * len(copies(0))
 
     def body(main_ref, stat_ref, out_ref):
         peaks, totals = [], []
@@ -154,11 +196,14 @@
             value = main_ref[b, 0:n_heads, :]
             acc = acc + jnp.dot(high, value, preferred_element_type=jnp.float32)
             acc = acc + jnp.dot(low, value, preferred_element_type=jnp.float32)
-        out_ref[...] = acc.astype(jnp.bfloat16)
+        rotated = acc.astype(jnp.bfloat16)
+        for h in range(n_target):
+            for spot in copies(h):
+                out_ref[spot] = rotated[h * heads_out : (h + 1) * heads_out]
 
     return pl.pallas_call(
         body,
-        out_shape=jax.ShapeDtypeStruct((n_heads, depth), jnp.bfloat16),
+        out_shape=jax.ShapeDtypeStruct((n_out, heads_out, depth), jnp.bfloat16),
         in_specs=[pl.BlockSpec(memory_space=VMEM)] * 2,
         out_specs=pl.BlockSpec(memory_space=VMEM),
         compiler_params=pltpu.CompilerParams(vmem_limit_bytes=16 * MIB),
@@ -166,64 +211,62 @@
     )(main, stats)
 
 
-def project(own_share, rows, wo, n_block, n_share):
+def project(own_share, rows, early, wo, n_block, tiles, spot):
     n_all, heads_here, _ = rows.shape
-    depth = wo.shape[0]
-    block_cols = wo.shape[1] // n_block
-    piece = block_cols // n_share
-    n_rows = n_all // n_share
-
-    def body(own_ref, x_ref, wo_ref, out_ref, weights, wide, packed, sem):
-        start = own_ref[0] * piece
-
-        def fetch(b):
-            cols = pl.ds(pl.multiple_of(b * block_cols + start, 128), piece)
-            return pltpu.make_async_copy(wo_ref.at[:, cols], weights.at[b], sem.at[b])
-
-        for b in range(n_block):
-            fetch(b).start()
+    n_early, depth, piece = early.shape
+    n_late = n_block - n_early
+    n_rows = n_all // len(tiles)
+
+    def body(own_ref, x_ref, early_ref, wo_ref, out_ref, late, wide, packed, sem):
+        fetch = weight_fetch(wo_ref, late, sem, own_ref[0], n_block, piece)
+        fetch_wo = [fetch(n_early + b, b) for b in range(n_late)]
+        for copy in fetch_wo:
+            copy.start()
         wide[...] = x_ref[...].astype(jnp.float32).reshape(n_all * heads_here, HD)
         for j in range(heads_here):
             pieces = [
-                wide[pl.ds(s * heads_here + j, n_rows, stride=heads_here * n_share), :]
-                for s in range(n_share)
+                wide[pl.ds(first * heads_here + j, n_rows, stride=heads_here * step), :]
+                for first, step in tiles
             ]
             packed[:, HD * j : HD * (j + 1)] = jnp.concatenate(pieces, axis=0).astype(jnp.bfloat16)
         x = packed[...]
         for b in range(n_block):
-            fetch(b).wait()
-            share = jnp.dot(x, weights[b], preferred_element_type=jnp.float32)
-            for s in range(n_share):
-                out_ref[b * n_share + s] = share[s * n_rows : (s + 1) * n_rows].astype(jnp.bfloat16)
-
+            if b < n_early:
+                block = early_ref[b]
+            else:
+                fetch_wo[b - n_early].wait()
+                block = late[b - n_early]
+            share = jnp.dot(x, block, preferred_element_type=jnp.float32)
+            for s in range(len(tiles)):
+                out_ref[spot(b, s)] = share[s * n_rows : (s + 1) * n_rows].astype(jnp.bfloat16)
+
+    in_vmem = pl.BlockSpec(memory_space=VMEM)
     return pl.pallas_call(
         body,
-        out_shape=jax.ShapeDtypeStruct((n_block * n_share, n_rows, piece), jnp.bfloat16),
+        out_shape=jax.ShapeDtypeStruct((n_block * len(tiles), n_rows, piece), jnp.bfloat16),
         in_specs=[
-            pl.BlockSpec(memory_space=SMEM),
-            pl.BlockSpec(memory_space=VMEM),
-            pl.BlockSpec(memory_space=pl.ANY),
+            pl.BlockSpec(memory_space=SMEM), in_vmem, in_vmem, pl.BlockSpec(memory_space=HBM)
         ],
-        out_specs=pl.BlockSpec(memory_space=VMEM),
+        out_specs=in_vmem,
         scratch_shapes=[
-            pltpu.VMEM((n_block, depth, piece), wo.dtype),
+            pltpu.VMEM((n_late, depth, piece), wo.dtype),
             pltpu.VMEM((n_all * heads_here, HD), jnp.float32),
             pltpu.VMEM((n_all, heads_here * HD), jnp.bfloat16),
-            pltpu.SemaphoreType.DMA((n_block,)),
+            pltpu.SemaphoreType.DMA((n_late,)),
         ],
-        compiler_params=pltpu.CompilerParams(vmem_limit_bytes=44 * MIB),
+        compiler_params=pltpu.CompilerParams(vmem_limit_bytes=24 * MIB),
         name="project",
-    )(own_share, rows, wo)
-
-
-def finish(shares, scales, residual, n_share):
-    n_all, n_rows, piece = shares.shape
+    )(own_share, rows, early, wo)
+
+
+def finish(shares, scales, residual, n_head, n_share, spot):
+    piece = shares.shape[2]
 
     def body(share_ref, scale_ref, res_ref, out_ref):
         for s in range(n_share):
-            total = share_ref[s].astype(jnp.float32)
-            for h in range(1, n_all // n_share):
-                total = total + share_ref[h * n_share + s].astype(jnp.float32)
+            total = share_ref[spot(0, s)].astype(jnp.float32)
+            for h in range(1, n_head):
+                total = total + share_ref[spot(h, s)].astype(jnp.float32)
             cols = slice(s * piece, (s + 1) * piece)
             out_ref[:, cols] = (
                 res_ref[:, cols].astype(jnp.float32) + total * scale_ref[:, cols]
@@ -247,48 +290,64 @@
     queries, new_kv, positions, lengths, kv_codes, kv_scales, wo_codes, wo_scales, residual
 ):
     n_head = lax.axis_size("head")
-    n_share = lax.axis_size("dp")
+    n_dp = lax.axis_size("dp")
     my_head = lax.axis_index("head")
-    my_share = lax.axis_index("dp")
     n_rows, width = queries.shape
     heads_here = width // HD
     n_heads = heads_here * n_head
     n_kv = new_kv.shape[2] // HD
     block_len = kv_codes.shape[2]
     own_cols = wo_codes.shape[1] // n_head
+    n_group = lax.axis_size("group")
+    if own_cols % (n_group * n_dp * 128):
+        n_group = 1
+    n_share = n_group * n_dp
+    piece = own_cols // n_share
+    my_share = lax.axis_index("dp")
+    axes = ("head", "dp")
+    if n_group > 1:
+        my_share = my_share + n_dp * lax.axis_index("group")
+        axes = ("group", "head", "dp")
+
+    def spot(head, share):
+        return (share // n_dp * n_head + head) * n_dp + share % n_dp
 
     gathered = exchange(jnp.broadcast_to(queries, (n_head, n_rows, width)), "head")
     cosine, sine = rotary_tables(positions)
     spread = jnp.repeat(jnp.swapaxes(kv_scales, 2, 3), n_heads // n_kv, axis=3)
-    scalars = jnp.concatenate([lengths, (my_head * block_len).reshape(1)]).astype(jnp.int32)
-    partial = attend(
-        scalars, gathered, cosine, sine, new_kv, kv_codes, spread[:, 0], spread[:, 1]
+    own_share = my_share.reshape(1).astype(jnp.int32)
+    first_slot = (my_head * block_len).reshape(1).astype(jnp.int32)
+    scalars, own_share, gathered, cosine, sine, spread = lax.optimization_barrier(
+        (jnp.concatenate([lengths, first_slot, own_share]), own_share, gathered, cosine, sine, spread)
+    )
+    partial, early = attend(
+        scalars, gathered, cosine, sine, new_kv, kv_codes, spread[:, 0], spread[:, 1], wo_codes,
+        n_head // 2, piece,
     )
 
     cuts = max(1, n_head // n_rows)
     depth = HD // cuts
     if cuts == 1:
         main = exchange(partial, "head")
-        rotated = settle(main, main, n_heads, n_heads)
+        stats, stat_row = main, n_heads
     else:
         values = partial[:, :n_heads].reshape(n_rows, n_heads, cuts, depth).swapaxes(1, 2)
         stats = partial[:, n_heads:].reshape(n_rows, 1, STAT_ROWS * cuts, depth)
         stats = jnp.broadcast_to(stats, (n_rows, cuts) + stats.shape[2:])
         message = jnp.concatenate([values, stats], axis=2)
         received = exchange(message.reshape((n_head,) + message.shape[2:]), "head")
-        rotated = settle(
-            received[:, :n_heads], received[:, n_heads:].reshape(n_head, STAT_ROWS, HD), n_heads, 0
-        )
-    copies = jnp.broadcast_to(
-        rotated.reshape(n_head, 1, heads_here, depth), (n_head, n_share, heads_here, depth)
-    )
-    rows = exchange(copies.reshape(n_head * n_share, heads_here, depth), ("head", "dp"))
+        main, stat_row = received[:, :n_heads], 0
+        stats = received[:, n_heads:].reshape(n_head, STAT_ROWS, HD)
+    copies = settle(
+        main, stats, n_heads, stat_row, n_head, lambda h: [spot(h, s) for s in range(n_share)]
+    )
+    rows = exchange(copies, axes)
     if cuts > 1:
-        rows = rows.reshape(n_rows, cuts, n_share, heads_here, depth).transpose(0, 2, 3, 1, 4)
-        rows = rows.reshape(n_rows * n_share, heads_here, HD)
-    shares = exchange(
-        project(my_share.reshape(1).astype(jnp.int32), rows, wo_codes, n_head, n_share), ("head", "dp"))
-    return finish(shares, wo_scales.reshape(1, own_cols), residual, n_share)
+        rows = rows.reshape(n_group, n_rows, cuts, n_dp, heads_here, depth)
+        rows = rows.transpose(0, 1, 3, 4, 2, 5).reshape(n_rows * n_share, heads_here, HD)
+    tiles = [(s // n_dp * n_rows * n_dp + s % n_dp, n_dp) for s in range(n_share)]
+    shares = exchange(project(own_share, rows, early, wo_codes, n_head, tiles, spot), axes)
+    return finish(shares, wo_scales.reshape(1, own_cols), residual, n_head, n_share, spot)
 
 
 def solution(mesh):

time: 73 us -> 69.8 us (0.956)
  blocking collectives: 26 us -> 35.9 us
  waiting for transfers between devices: 12.8 us -> 7.33 us
  starting transfers between devices: 10.8 us -> 7.28 us
  Pallas kernels: 15.6 us -> 12.4 us
  local copies, waits for them, and re-layouts: 5.47 us -> 4.7 us
    all_to_all x2 -> x3, blocking collectives: 26 us -> 35.9 us  [exchange(): return lax.all_to_all(block, axes, split_axis=0, concat_axis=0, tiled=True)]
    all_to_all x2 -> x1, waiting for transfers between devices: 12.8 us -> 7.33 us  [exchange(): return lax.all_to_all(block, axes, split_axis=0, concat_axis=0, tiled=True)]
    all_to_all x2 -> x1, starting transfers between devices: 10.8 us -> 7.28 us  [exchange(): return lax.all_to_all(block, axes, split_axis=0, concat_axis=0, tiled=True)]
    pallas_call x3, Pallas kernels: 15 us -> 11.8 us  [the longest x1 6.02 us: attend(): pl.pallas_call(body, out_shape=(jax.ShapeDtypeStruct((n_rows, n_heads + S...]
    unnamed x10 -> x8, local copies, waits for them, and re-layouts: 2.33 us -> 1.98 us
  transfers between devices with their start and end apart: 2 -> 1, of which waited for: 2 -> 1; matrix products, arithmetic and copies ran while one was open for 4% -> 2% of each run, Pallas kernels for 0% -> 0%
where the time goes in v2:
time: 69.8 us; the launch traced here: 69.3 us
  blocking collectives  35.9 us (51%)
  Pallas kernels  12.4 us (18%)
  waiting for transfers between devices  7.33 us (11%)
  starting transfers between devices  7.28 us (10%)
  local copies, waits for them, and re-layouts  4.7 us (7%)
  other arithmetic  1.58 us (2%)
    all_to_all x3, blocking collectives, exchange(): return lax.all_to_all(block, axes, split_axis=0, concat_axis=0, tiled=True)  35.9 us
    all_to_all x1, waiting for transfers between devices, exchange(): return lax.all_to_all(block, axes, split_axis=0, concat_axis=0, tiled=True)  7.33 us
    all_to_all x1, starting transfers between devices, exchange(): return lax.all_to_all(block, axes, split_axis=0, concat_axis=0, tiled=True)  7.28 us
    pallas_call x1, Pallas kernels, attend(): pl.pallas_call(body, out_shape=(jax.ShapeDtypeStruct((n_rows, n_heads + S...  6.02 us
    pallas_call x1, Pallas kernels, project(): pl.pallas_call(body, out_shape=jax.ShapeDtypeStruct((n_block * len(tiles)...  5.42 us
    unnamed x8, local copies, waits for them, and re-layouts  1.98 us
    broadcast_in_dim x1, local copies, waits for them, and re-layouts, on_device(): jnp.broadcast_to(queries, (n_head, n_rows, width))  1.47 us
  transfers between devices with their start and end apart: 1, of which 1 were waited for; matrix products, arithmetic and copies ran while one was open for 2% of the time, Pallas kernels for 0%

profile of v2, /device:TPU:0, one launch (start us, length us, event | category | flops | bytes accessed | tf_op | source)
XLA Modules:
  0.0 69.3 jit_solution(6795441513421556729)
XLA Ops:
  0.0 1.5 %broadcast_in_dim.8 = bf16[8,8,2048]{2,1,0:T(8,128)(2,1)} broadcast(bf16[8,2048]{1,0:T(8,128)(2,1)} %param.9), dimensions={1,2} | broadcast | bytes 294912 | tf_op jit(solution)/shard_map/broadcast_in_dim | solution.py:315
  1.5 7.3 %all-to-all-start = ((bf16[8,8,2048]{2,1,0:T(8,128)(2,1)}), bf16[8,8,2048]{2,1,0:T(8,128)(2,1)S(1)}, u32[]{:S(2)}, u32[]{:S(2)}) async-start(bf16[8,8,2048]{2,1,0:T(8,128)(2,1)} %broadcast_in_dim.8), calls=%async_computation | async-start | bytes 524288 | tf_op jit(solution)/shard_map/all_to_all | solution.py:286
  8.8 0.7 convert_element_type.3
  9.4 0.7 %pad_add_fusion.s_ref = s32[10]{0:T(128)S(1)} fusion(s32[1]{0:T(128)} %bitcast.1.own_ref, s32[1]{0:T(128)} %bitcast, s32[8]{0:T(128)} %param.12), kind=kLoop, calls=%fused_computation.7 | loop fusion | flops 20 | bytes 80 | tf_op jit(solution)/shard_map/concatenate | solution.py:321
  10.2 0.1 fusion
  10.3 0.1 pad_maximum_fusion
  10.3 7.3 %all-to-all-done.q_ref = bf16[8,8,2048]{2,1,0:T(8,128)(2,1)S(1)} async-done(((bf16[8,8,2048]{2,1,0:T(8,128)(2,1)}), bf16[8,8,2048]{2,1,0:T(8,128)(2,1)S(1)}, u32[]{:S(2)}, u32[]{:S(2)}) %all-to-all-start) | async-done | bytes 262176 | tf_op jit(solution)/shard_map/all_to_all | solution.py:286
  17.7 0.9 %broadcast_in_dim.9 = f32[8,2,32,8,16]{2,4,3,1,0:T(8,128)S(1)} broadcast(f32[8,2,32,8]{2,3,1,0:T(8,128)} %bitcast.11), dimensions={0,1,2,3} | broadcast | bytes 278528 | tf_op jit(solution)/shard_map/broadcast_in_dim | solution.py:317
  18.6 0.3 copy.11
  18.9 0.0 copy-start
  18.9 1.2 %copy-done = bf16[8,2,32,1024]{3,2,1,0:T(8,128)(2,1)S(1)} copy-done((bf16[8,2,32,1024]{3,2,1,0:T(8,128)(2,1)S(1)}, bf16[8,2,32,1024]{3,2,1,0:T(8,128)(2,1)}, u32[]{:S(2)}) %copy-start) | copy-done | bytes 1048600
  20.2 0.0 copy-start.1
  20.2 0.8 %copy-done.1 = bf16[8,2,1024]{2,1,0:T(2,128)(2,1)S(1)} copy-done((bf16[8,2,1024]{2,1,0:T(2,128)(2,1)S(1)}, bf16[8,2,1024]{2,1,0:T(2,128)(2,1)}, u32[]{:S(2)}) %copy-start.1) | copy-done | bytes 32792
  20.9 0.0 copy-start.2
  20.9 0.0 copy-start.3
  20.9 6.0 %attend.1 = (bf16[8,136,128]{2,1,0:T(8,128)(2,1)S(1)}, bf16[4,2048,512]{2,1,0:T(8,128)(2,1)S(1)}) custom-call(s32[10]{0:T(128)S(1)} %pad_add_fusion.s_ref, bf16[8,8,2048]{2,1,0:T(8,128)(2,1)S(1)} %all-to-all-done.q_ref, f32[8,128]{1,0:T(8,128)S(1)} %get-tuple-element.16.cos_ref, f32[8,128]{1,0:T(8,128)S(1)} %get-tuple-element.17.sin_ref, ...), custom_call_target="tpu_custom_call" | custom-call | tf_op jit(solution)/shard_map/attend/pallas_call | solution.py:144
  26.9 13.1 %all_to_all.20.main_ref.stat_ref = bf16[8,136,128]{2,1,0:T(8,128)(2,1)S(1)} all-to-all(bf16[8,136,128]{2,1,0:T(8,128)(2,1)S(1)} %get-tuple-element.19), channel_id=1, replica_groups=mesh['group'=2,'head'=8,'dp'=2] {'head'}, dimensions={0} | all-to-all | bytes 557056 | tf_op jit(solution)/shard_map/all_to_all | solution.py:286
  40.1 0.3 settle.1
  40.4 10.8 %all_to_all.21.x_ref = bf16[32,16,128]{2,1,0:T(8,128)(2,1)S(1)} all-to-all(bf16[32,16,128]{2,1,0:T(8,128)(2,1)S(1)} %settle.1), channel_id=1, replica_groups=mesh['group'=2,'head'=8,'dp'=2] {'group','head','dp'}, dimensions={0} | all-to-all | bytes 262144 | tf_op jit(solution)/shard_map/all_to_all | solution.py:286
  51.2 5.4 %project.1 = bf16[32,8,512]{2,1,0:T(8,128)(2,1)S(1)} custom-call(s32[1]{0:T(128)} %bitcast.1.own_ref, bf16[32,16,128]{2,1,0:T(8,128)(2,1)S(1)} %all_to_all.21.x_ref, bf16[4,2048,512]{2,1,0:T(8,128)(2,1)S(1)} %get-tuple-element.20.early_ref, bf16[2048,16384]{1,0:T(8,128)(2,1)} %wo_ref.3), custom_call_target="tpu_custom_call" | custom-call | tf_op jit(solution)/shard_map/project/pallas_call | solution.py:244
  56.7 12.0 %all_to_all.22.share_ref = bf16[32,8,512]{2,1,0:T(8,128)(2,1)S(1)} all-to-all(bf16[32,8,512]{2,1,0:T(8,128)(2,1)S(1)} %project.1), channel_id=1, replica_groups=mesh['group'=2,'head'=8,'dp'=2] {'group','head','dp'}, dimensions={0} | all-to-all | bytes 524288 | tf_op jit(solution)/shard_map/all_to_all | solution.py:286
  68.7 0.0 copy-done.2
  68.7 0.0 copy-done.3
  68.7 0.7 finish.1
  (2 shorter events, 0.0 us)
Async XLA Ops:
  1.5 16.2 %all-to-all-start = ((bf16[8,8,2048]{2,1,0:T(8,128)(2,1)}), bf16[8,8,2048]{2,1,0:T(8,128)(2,1)S(1)}, u32[]{:S(2)}, u32[]{:S(2)}) async-start(bf16[8,8,2048]{2,1,0:T(8,128)(2,1)} %broadcast_in_dim.8), calls=%async_computation | async-start | bytes 524288 | tf_op jit(solution)/shard_map/all_to_all | solution.py:286
  18.9 1.2 %copy-start = (bf16[8,2,32,1024]{3,2,1,0:T(8,128)(2,1)S(1)}, bf16[8,2,32,1024]{3,2,1,0:T(8,128)(2,1)}, u32[]{:S(2)}) copy-start(bf16[8,2,32,1024]{3,2,1,0:T(8,128)(2,1)} %kv_hbm.1) | copy-start | bytes 3145732
  20.2 0.8 %copy-start.1 = (bf16[8,2,1024]{2,1,0:T(2,128)(2,1)S(1)}, bf16[8,2,1024]{2,1,0:T(2,128)(2,1)}, u32[]{:S(2)}) copy-start(bf16[8,2,1024]{2,1,0:T(2,128)(2,1)} %new_hbm.1) | copy-start | bytes 98308
  20.9 47.7 %copy-start.2 = (bf16[8,2048]{1,0:T(8,128)(2,1)S(1)}, bf16[8,2048]{1,0:T(8,128)(2,1)}, u32[]{:S(2)}) copy-start(bf16[8,2048]{1,0:T(8,128)(2,1)} %res_ref.1) | copy-start | bytes 98308
  20.9 47.7 %copy-start.3 = (f32[2048]{0:T(1024)S(1)}, f32[2048]{0:T(1024)}, u32[]{:S(2)}) copy-start(f32[2048]{0:T(1024)} %param.16) | copy-start | bytes 24580

commit v3 on v2

--- a/solution.py
+++ b/solution.py
@@ -28,6 +28,10 @@
     return lax.dot_general(left, right, (dims, ((), ())), preferred_element_type=jnp.float32)
 
 
+def in_place(array):
+    return pltpu.with_memory_space_constraint(array, HBM)
+
+
 def rotary_tables(positions):
     half_dim = HD // 2
     inverse_rate = ROPE_BASE ** (-(jnp.arange(half_dim, dtype=jnp.float32) * (2.0 / HD)))
@@ -37,17 +41,31 @@
     return jnp.concatenate([cosine, cosine], -1), jnp.concatenate([-sine, sine], -1)
 
 
-def weight_fetch(wo_ref, out_ref, sem, share, n_block, piece):
-    def fetch(block, slot):
-        start = block * (wo_ref.shape[1] // n_block) + share * piece
-        cols = pl.ds(pl.multiple_of(start, 128), piece)
-        return pltpu.make_async_copy(wo_ref.at[:, cols], out_ref.at[slot], sem.at[slot])
-
-    return fetch
+def stage(arrays):
+    def body(*refs):
+        count = len(arrays)
+        copies = [
+            pltpu.make_async_copy(refs[n], refs[count + n], refs[-1].at[n]) for n in range(count)
+        ]
+        for copy in copies:
+            copy.start()
+        for copy in copies:
+            copy.wait()
+
+    in_hbm, in_vmem = pl.BlockSpec(memory_space=HBM), pl.BlockSpec(memory_space=VMEM)
+    return pl.pallas_call(
+        body,
+        out_shape=tuple(pltpu.VMEM(a.shape, a.dtype) for a in arrays),
+        in_specs=[in_hbm] * len(arrays),
+        out_specs=(in_vmem,) * len(arrays),
+        scratch_shapes=[pltpu.SemaphoreType.DMA((len(arrays),))],
+        compiler_params=pltpu.CompilerParams(vmem_limit_bytes=MIB // 4),
+        name="stage",
+    )(*[in_place(a) for a in arrays])
 
 
 def attend(
-    scalars, gathered, cosine, sine, new_kv, kv_codes, key_scales, value_scales, wo, n_early, piece
+    scalars, gathered, cosine, sine, new_kv, kv_codes, key_scales, value_scales
 ):
     n_src, n_rows, width = gathered.shape
     heads_here = width // HD
@@ -57,21 +75,7 @@
     group = n_heads // n_kv
     score_scale = HD ** (-0.5)
 
-    def body(
-        s_ref, q_ref, cos_ref, sin_ref, new_hbm, kv_hbm, ks_ref, vs_ref, wo_ref, out_ref, early_ref,
-        qs, ks, new_ref, kv_ref, new_sem, kv_sem, wo_sem,
-    ):
-        fetch_new = pltpu.make_async_copy(new_hbm, new_ref, new_sem)
-        fetch_new.start()
-        fetch_kv = [
-            pltpu.make_async_copy(kv_hbm.at[r], kv_ref.at[r], kv_sem.at[r]) for r in range(n_rows)
-        ]
-        for copy in fetch_kv:
-            copy.start()
-        fetch = weight_fetch(wo_ref, early_ref, wo_sem, s_ref[n_rows + 1], n_src, piece)
-        fetch_wo = [fetch(b, b) for b in range(n_early)]
-        for copy in fetch_wo:
-            copy.start()
+    def body(s_ref, q_ref, cos_ref, sin_ref, new_ref, kv_ref, ks_ref, vs_ref, out_ref, qs, ks):
         cos, sin = cos_ref[...], sin_ref[...]
 
         def rotate(tile):
@@ -82,7 +86,6 @@
             for j in range(heads_here):
                 head = src * heads_here + j
                 qs[n_rows * head : n_rows * (head + 1), :] = rotate(block[:, HD * j : HD * (j + 1)])
-        fetch_new.wait()
         fresh = new_ref[:, 0, :].astype(jnp.float32)
         for k in range(n_kv):
             ks[n_rows * k : n_rows * (k + 1), :] = rotate(fresh[:, HD * k : HD * (k + 1)])
@@ -93,7 +96,6 @@
         slot = first_slot + lax.broadcasted_iota(jnp.int32, (block_len, n_heads), 0)
         own_kv = lax.broadcasted_iota(jnp.int32, (n_kv, n_heads), 0) == lane_group
         for r in range(n_rows):
-            fetch_kv[r].wait()
             query = qs[pl.ds(r, n_heads, stride=n_rows), :].astype(jnp.bfloat16)
             keys = jnp.concatenate(
                 [kv_ref[r, 0, :, HD * k : HD * (k + 1)] for k in range(n_kv)], axis=0
@@ -137,31 +139,20 @@
             pad = jnp.zeros((STAT_ROWS - len(parts), n_heads), jnp.float32)
             stats = jnp.concatenate([part.astype(jnp.float32) for part in parts] + [pad], axis=0)
             out_ref[r, n_heads : n_heads + STAT_ROWS, :] = stats.astype(jnp.bfloat16)
-        for copy in fetch_wo:
-            copy.wait()
-
-    in_vmem, in_hbm = pl.BlockSpec(memory_space=VMEM), pl.BlockSpec(memory_space=HBM)
-    return pl.pallas_call(
-        body,
-        out_shape=(
-            jax.ShapeDtypeStruct((n_rows, n_heads + STAT_ROWS, HD), jnp.bfloat16),
-            pltpu.VMEM((n_early, wo.shape[0], piece), wo.dtype),
-        ),
-        in_specs=[pl.BlockSpec(memory_space=SMEM)]
-        + [in_vmem] * 3 + [in_hbm] * 2 + [in_vmem] * 2 + [in_hbm],
-        out_specs=(in_vmem, in_vmem),
+
+    in_vmem = pl.BlockSpec(memory_space=VMEM)
+    return pl.pallas_call(
+        body,
+        out_shape=jax.ShapeDtypeStruct((n_rows, n_heads + STAT_ROWS, HD), jnp.bfloat16),
+        in_specs=[pl.BlockSpec(memory_space=SMEM)] + [in_vmem] * 7,
+        out_specs=in_vmem,
         scratch_shapes=[
             pltpu.VMEM((n_rows * n_heads, HD), jnp.float32),
             pltpu.VMEM((n_rows * n_kv, HD), jnp.float32),
-            pltpu.VMEM(new_kv.shape, new_kv.dtype),
-            pltpu.VMEM(kv_codes.shape, kv_codes.dtype),
-            pltpu.SemaphoreType.DMA,
-            pltpu.SemaphoreType.DMA((n_rows,)),
-            pltpu.SemaphoreType.DMA((n_early,)),
         ],
-        compiler_params=pltpu.CompilerParams(vmem_limit_bytes=12 * MIB),
+        compiler_params=pltpu.CompilerParams(vmem_limit_bytes=6 * MIB),
         name="attend",
-    )(scalars, gathered, cosine, sine, new_kv, kv_codes, key_scales, value_scales, wo)
+    )(scalars, gathered, cosine, sine, new_kv, kv_codes, key_scales, value_scales)
 
 
 def settle(main, stats, n_heads, stat_row, n_target, copies):
@@ -211,17 +202,20 @@
     )(main, stats)
 
 
-def project(own_share, rows, early, wo, n_block, tiles, spot):
+def project(own_share, rows, wo, n_block, tiles, spot):
     n_all, heads_here, _ = rows.shape
-    n_early, depth, piece = early.shape
-    n_late = n_block - n_early
+    depth = wo.shape[0]
+    block_cols = wo.shape[1] // n_block
+    piece = block_cols // len(tiles)
     n_rows = n_all // len(tiles)
 
-    def body(own_ref, x_ref, early_ref, wo_ref, out_ref, late, wide, packed, sem):
-        fetch = weight_fetch(wo_ref, late, sem, own_ref[0], n_block, piece)
-        fetch_wo = [fetch(n_early + b, b) for b in range(n_late)]
-        for copy in fetch_wo:
-            copy.start()
+    def body(own_ref, x_ref, wo_ref, out_ref, weights, wide, packed, sem):
+        def fetch(b):
+            cols = pl.ds(pl.multiple_of(b * block_cols + own_ref[0] * piece, 128), piece)
+            return pltpu.make_async_copy(wo_ref.at[:, cols], weights.at[b], sem.at[b])
+
+        for b in range(n_block):
+            fetch(b).start()
         wide[...] = x_ref[...].astype(jnp.float32).reshape(n_all * heads_here, HD)
         for j in range(heads_here):
             pieces = [
@@ -231,12 +225,8 @@
             packed[:, HD * j : HD * (j + 1)] = jnp.concatenate(pieces, axis=0).astype(jnp.bfloat16)
         x = packed[...]
         for b in range(n_block):
-            if b < n_early:
-                block = early_ref[b]
-            else:
-                fetch_wo[b - n_early].wait()
-                block = late[b - n_early]
-            share = jnp.dot(x, block, preferred_element_type=jnp.float32)
+            fetch(b).wait()
+            share = jnp.dot(x, weights[b], preferred_element_type=jnp.float32)
             for s in range(len(tiles)):
                 out_ref[spot(b, s)] = share[s * n_rows : (s + 1) * n_rows].astype(jnp.bfloat16)
 
@@ -244,19 +234,17 @@
     return pl.pallas_call(
         body,
         out_shape=jax.ShapeDtypeStruct((n_block * len(tiles), n_rows, piece), jnp.bfloat16),
-        in_specs=[
-            pl.BlockSpec(memory_space=SMEM), in_vmem, in_vmem, pl.BlockSpec(memory_space=HBM)
-        ],
+        in_specs=[pl.BlockSpec(memory_space=SMEM), in_vmem, pl.BlockSpec(memory_space=HBM)],
         out_specs=in_vmem,
         scratch_shapes=[
-            pltpu.VMEM((n_late, depth, piece), wo.dtype),
+            pltpu.VMEM((n_block, depth, piece), wo.dtype),
             pltpu.VMEM((n_all * heads_here, HD), jnp.float32),
             pltpu.VMEM((n_all, heads_here * HD), jnp.bfloat16),
-            pltpu.SemaphoreType.DMA((n_late,)),
+            pltpu.SemaphoreType.DMA((n_block,)),
         ],
         compiler_params=pltpu.CompilerParams(vmem_limit_bytes=24 * MIB),
         name="project",
-    )(own_share, rows, early, wo)
+    )(own_share, rows, in_place(wo))
 
 
 def finish(shares, scales, residual, n_head, n_share, spot):
@@ -317,13 +305,12 @@
     spread = jnp.repeat(jnp.swapaxes(kv_scales, 2, 3), n_heads // n_kv, axis=3)
     own_share = my_share.reshape(1).astype(jnp.int32)
     first_slot = (my_head * block_len).reshape(1).astype(jnp.int32)
-    scalars, own_share, gathered, cosine, sine, spread = lax.optimization_barrier(
-        (jnp.concatenate([lengths, first_slot, own_share]), own_share, gathered, cosine, sine, spread)
+    scalars = jnp.concatenate([lengths, first_slot])
+    new_staged, kv_staged = stage((new_kv, kv_codes))
+    partial = attend(
+        scalars, gathered, cosine, sine, new_staged, kv_staged, spread[:, 0], spread[:, 1]
     )
-    partial, early = attend(
-        scalars, gathered, cosine, sine, new_kv, kv_codes, spread[:, 0], spread[:, 1], wo_codes,
-        n_head // 2, piece,
-    )
+    own_share, partial = lax.optimization_barrier((own_share, partial))
 
     cuts = max(1, n_head // n_rows)
     depth = HD // cuts
@@ -346,7 +333,7 @@
         rows = rows.reshape(n_group, n_rows, cuts, n_dp, heads_here, depth)
         rows = rows.transpose(0, 1, 3, 4, 2, 5).reshape(n_rows * n_share, heads_here, HD)
     tiles = [(s // n_dp * n_rows * n_dp + s % n_dp, n_dp) for s in range(n_share)]
-    shares = exchange(project(own_share, rows, early, wo_codes, n_head, tiles, spot), axes)
+    shares = exchange(project(own_share, rows, wo_codes, n_head, tiles, spot), axes)
     return finish(shares, wo_scales.reshape(1, own_cols), residual, n_head, n_share, spot)
 
 

time: 69.8 us -> 64.7 us (0.927)
  waiting for transfers between devices: 7.33 us -> 4.69 us
  local copies, waits for them, and re-layouts: 4.7 us -> 2.82 us
    all_to_all x1, waiting for transfers between devices: 7.33 us -> 4.69 us  [exchange(): return lax.all_to_all(block, axes, split_axis=0, concat_axis=0, tiled=True)]
    unnamed x8 -> x6, local copies, waits for them, and re-layouts: 1.98 us -> 0.35 us
    pallas_call x1 -> x2, Pallas kernels: 6.02 us -> 4.4 us  [the longest x1 3.13 us: attend(): pl.pallas_call(body, out_shape=jax.ShapeDtypeStruct((n_rows, n_heads + ST...]
    pallas_call x1, Pallas kernels: 5.42 us -> 6.51 us  [project(): pl.pallas_call(body, out_shape=jax.ShapeDtypeStruct((n_block * len(tiles)...]
  transfers between devices with their start and end apart: 1 -> 1, of which waited for: 1 -> 1; matrix products, arithmetic and copies ran while one was open for 2% -> 5% of each run, Pallas kernels for 0% -> 2%
where the time goes in v3:
time: 64.7 us; the launch traced here: 64.3 us
  blocking collectives  35.9 us (55%)
  Pallas kernels  11.9 us (18%)
  starting transfers between devices  7.28 us (11%)
  waiting for transfers between devices  4.69 us (7%)
  local copies, waits for them, and re-layouts  2.82 us (4%)
  other arithmetic  1.59 us (2%)
    all_to_all x3, blocking collectives, exchange(): return lax.all_to_all(block, axes, split_axis=0, concat_axis=0, tiled=True)  35.9 us
    all_to_all x1, starting transfers between devices, exchange(): return lax.all_to_all(block, axes, split_axis=0, concat_axis=0, tiled=True)  7.28 us
    pallas_call x1, Pallas kernels, project(): pl.pallas_call(body, out_shape=jax.ShapeDtypeStruct((n_block * len(tiles)...  6.51 us
    all_to_all x1, waiting for transfers between devices, exchange(): return lax.all_to_all(block, axes, split_axis=0, concat_axis=0, tiled=True)  4.69 us
    pallas_call x1, Pallas kernels, attend(): pl.pallas_call(body, out_shape=jax.ShapeDtypeStruct((n_rows, n_heads + ST...  3.13 us
    broadcast_in_dim x1, local copies, waits for them, and re-layouts, on_device(): jnp.broadcast_to(queries, (n_head, n_rows, width))  1.49 us
  transfers between devices with their start and end apart: 1, of which 1 were waited for; matrix products, arithmetic and copies ran while one was open for 5% of the time, Pallas kernels for 2%

profile of v3, /device:TPU:0, one launch (start us, length us, event | category | flops | bytes accessed | tf_op | source)
XLA Modules:
  0.0 64.3 jit_solution(12339887224592370680)
XLA Ops:
  0.0 0.0 copy-start.1
  0.0 0.0 copy-start
  0.0 1.5 %broadcast_in_dim.8 = bf16[8,8,2048]{2,1,0:T(8,128)(2,1)} broadcast(bf16[8,2048]{1,0:T(8,128)(2,1)} %param.9), dimensions={1,2} | broadcast | bytes 294912 | tf_op jit(solution)/shard_map/broadcast_in_dim | solution.py:303
  1.5 7.3 %all-to-all-start = ((bf16[8,8,2048]{2,1,0:T(8,128)(2,1)}), bf16[8,8,2048]{2,1,0:T(8,128)(2,1)S(1)}, u32[]{:S(2)}, u32[]{:S(2)}) async-start(bf16[8,8,2048]{2,1,0:T(8,128)(2,1)} %broadcast_in_dim.8), calls=%async_computation | async-start | bytes 524288 | tf_op jit(solution)/shard_map/all_to_all | solution.py:274
  8.8 0.9 %broadcast_in_dim.9 = f32[8,2,32,8,16]{2,4,3,1,0:T(8,128)S(1)} broadcast(f32[8,2,32,8]{2,3,1,0:T(8,128)} %bitcast.11), dimensions={0,1,2,3} | broadcast | bytes 278528 | tf_op jit(solution)/shard_map/broadcast_in_dim | solution.py:305
  9.7 0.1 fusion.1
  9.8 0.7 %convert_element_type.3 = f32[8]{0:T(128)S(1)} convert(s32[8]{0:T(128)} %param.11) | non-fusion elementwise | flops 8 | bytes 64 | tf_op jit(solution)/shard_map/convert_element_type | solution.py:38
  10.5 0.2 copy.13
  10.6 0.2 copy.14
  10.8 1.3 %stage.1 = (bf16[8,2,1024]{2,1,0:T(2,128)(2,1)S(1)}, bf16[8,2,32,1024]{3,2,1,0:T(8,128)(2,1)S(1)}) custom-call(bf16[8,2,1024]{2,1,0:T(2,128)(2,1)} %refs_0_.1, bf16[8,2,32,1024]{3,2,1,0:T(8,128)(2,1)} %refs_1_.1), custom_call_target="tpu_custom_call" | custom-call | tf_op jit(solution)/shard_map/stage/pallas_call | solution.py:56
  12.1 0.7 %pad_add_fusion.s_ref = s32[9]{0:T(128)S(1)} fusion(s32[1]{0:T(128)} %bitcast.1, s32[8]{0:T(128)} %param.12), kind=kLoop, calls=%fused_computation.5 | loop fusion | flops 9 | bytes 72 | tf_op jit(solution)/shard_map/concatenate | solution.py:308
  12.8 0.1 fusion
  12.9 0.1 pad_maximum_fusion
  13.0 4.7 %all-to-all-done.q_ref = bf16[8,8,2048]{2,1,0:T(8,128)(2,1)S(1)} async-done(((bf16[8,8,2048]{2,1,0:T(8,128)(2,1)}), bf16[8,8,2048]{2,1,0:T(8,128)(2,1)S(1)}, u32[]{:S(2)}, u32[]{:S(2)}) %all-to-all-start) | async-done | bytes 262176 | tf_op jit(solution)/shard_map/all_to_all | solution.py:274
  17.7 3.1 %attend.1 = bf16[8,136,128]{2,1,0:T(8,128)(2,1)S(1)} custom-call(s32[9]{0:T(128)S(1)} %pad_add_fusion.s_ref, bf16[8,8,2048]{2,1,0:T(8,128)(2,1)S(1)} %all-to-all-done.q_ref, f32[8,128]{1,0:T(8,128)S(1)} %get-tuple-element.18.cos_ref, f32[8,128]{1,0:T(8,128)S(1)} %get-tuple-element.19.sin_ref, bf16[8,2,1024]{2,1,0:T(2,128)(2,1)S(1)} %get-tuple-element.9.new_ref, ...), custom_call_target="tpu_custom_call" | custom-call | tf_op jit(solution)/shard_map/attend/pallas_call | solution.py:144
  20.8 13.1 %all_to_all.20.main_ref.stat_ref = bf16[8,136,128]{2,1,0:T(8,128)(2,1)S(1)} all-to-all(bf16[8,136,128]{2,1,0:T(8,128)(2,1)S(1)} %attend.1), channel_id=1, replica_groups=mesh['group'=2,'head'=8,'dp'=2] {'head'}, dimensions={0} | all-to-all | bytes 557056 | tf_op jit(solution)/shard_map/all_to_all | solution.py:274
  34.0 0.3 settle.1
  34.3 10.8 %all_to_all.21.x_ref = bf16[32,16,128]{2,1,0:T(8,128)(2,1)S(1)} all-to-all(bf16[32,16,128]{2,1,0:T(8,128)(2,1)S(1)} %settle.1), channel_id=1, replica_groups=mesh['group'=2,'head'=8,'dp'=2] {'group','head','dp'}, dimensions={0} | all-to-all | bytes 262144 | tf_op jit(solution)/shard_map/all_to_all | solution.py:274
  45.1 6.5 %project.1 = bf16[32,8,512]{2,1,0:T(8,128)(2,1)S(1)} custom-call(s32[1]{0:T(128)} %bitcast.own_ref, bf16[32,16,128]{2,1,0:T(8,128)(2,1)S(1)} %all_to_all.21.x_ref, bf16[2048,16384]{1,0:T(8,128)(2,1)} %wo_ref.1), custom_call_target="tpu_custom_call" | custom-call | tf_op jit(solution)/shard_map/project/pallas_call | solution.py:234
  51.7 12.0 %all_to_all.22.share_ref = bf16[32,8,512]{2,1,0:T(8,128)(2,1)S(1)} all-to-all(bf16[32,8,512]{2,1,0:T(8,128)(2,1)S(1)} %project.1), channel_id=1, replica_groups=mesh['group'=2,'head'=8,'dp'=2] {'group','head','dp'}, dimensions={0} | all-to-all | bytes 524288 | tf_op jit(solution)/shard_map/all_to_all | solution.py:274
  63.6 0.0 copy-done.1
  63.6 0.0 copy-done
  63.6 0.7 %finish.1 = bf16[8,2048]{1,0:T(8,128)(2,1)} custom-call(bf16[32,8,512]{2,1,0:T(8,128)(2,1)S(1)} %all_to_all.22.share_ref, f32[1,2048]{1,0:T(1,128)S(1)} %bitcast.9, bf16[8,2048]{1,0:T(8,128)(2,1)S(1)} %copy-done), custom_call_target="tpu_custom_call" | custom-call | tf_op jit(solution)/shard_map/finish/pallas_call | solution.py:263
  (1 shorter events, 0.0 us)
Async XLA Ops:
  0.0 63.6 %copy-start.1 = (f32[2048]{0:T(1024)S(1)}, f32[2048]{0:T(1024)}, u32[]{:S(2)}) copy-start(f32[2048]{0:T(1024)} %param.16) | copy-start | bytes 24580
  0.0 63.6 %copy-start = (bf16[8,2048]{1,0:T(8,128)(2,1)S(1)}, bf16[8,2048]{1,0:T(8,128)(2,1)}, u32[]{:S(2)}) copy-start(bf16[8,2048]{1,0:T(8,128)(2,1)} %res_ref.1) | copy-start | bytes 98308
  1.5 16.2 %all-to-all-start = ((bf16[8,8,2048]{2,1,0:T(8,128)(2,1)}), bf16[8,8,2048]{2,1,0:T(8,128)(2,1)S(1)}, u32[]{:S(2)}, u32[]{:S(2)}) async-start(bf16[8,8,2048]{2,1,0:T(8,128)(2,1)} %broadcast_in_dim.8), calls=%async_computation | async-start | bytes 524288 | tf_op jit(solution)/shard_map/all_to_all | solution.py:274

commit v4 on v2

--- a/solution.py
+++ b/solution.py
@@ -10,6 +10,8 @@
 ROPE_BASE = 500000.0
 NEG_FILL = -1e30
 STAT_ROWS = 8
+ROW_UNROLL = 4
+EARLY_EIGHTHS = 3
 MIB = 1 << 20
 VMEM = pltpu.MemorySpace.VMEM
 SMEM = pltpu.MemorySpace.SMEM
@@ -26,6 +28,10 @@
 
 def contract(left, right, dims):
     return lax.dot_general(left, right, (dims, ((), ())), preferred_element_type=jnp.float32)
+
+
+def in_place(array):
+    return pltpu.with_memory_space_constraint(array, HBM)
 
 
 def rotary_tables(positions):
@@ -35,6 +41,29 @@
     cosine = jnp.cos(angles)
     sine = jnp.sin(angles)
     return jnp.concatenate([cosine, cosine], -1), jnp.concatenate([-sine, sine], -1)
+
+
+def stage(arrays):
+    def body(*refs):
+        count = len(arrays)
+        copies = [
+            pltpu.make_async_copy(refs[n], refs[count + n], refs[-1].at[n]) for n in range(count)
+        ]
+        for copy in copies:
+            copy.start()
+        for copy in copies:
+            copy.wait()
+
+    in_hbm, in_vmem = pl.BlockSpec(memory_space=HBM), pl.BlockSpec(memory_space=VMEM)
+    return pl.pallas_call(
+        body,
+        out_shape=tuple(pltpu.VMEM(a.shape, a.dtype) for a in arrays),
+        in_specs=[in_hbm] * len(arrays),
+        out_specs=(in_vmem,) * len(arrays),
+        scratch_shapes=[pltpu.SemaphoreType.DMA((len(arrays),))],
+        compiler_params=pltpu.CompilerParams(vmem_limit_bytes=MIB // 4),
+        name="stage",
+    )(*[in_place(a) for a in arrays])
 
 
 def weight_fetch(wo_ref, out_ref, sem, share, n_block, piece):
@@ -58,16 +87,9 @@
     score_scale = HD ** (-0.5)
 
     def body(
-        s_ref, q_ref, cos_ref, sin_ref, new_hbm, kv_hbm, ks_ref, vs_ref, wo_ref, out_ref, early_ref,
-        qs, ks, new_ref, kv_ref, new_sem, kv_sem, wo_sem,
+        s_ref, q_ref, cos_ref, sin_ref, new_ref, kv_ref, ks_ref, vs_ref, wo_ref, out_ref, early_ref,
+        qs, ks, wo_sem,
     ):
-        fetch_new = pltpu.make_async_copy(new_hbm, new_ref, new_sem)
-        fetch_new.start()
-        fetch_kv = [
-            pltpu.make_async_copy(kv_hbm.at[r], kv_ref.at[r], kv_sem.at[r]) for r in range(n_rows)
-        ]
-        for copy in fetch_kv:
-            copy.start()
         fetch = weight_fetch(wo_ref, early_ref, wo_sem, s_ref[n_rows + 1], n_src, piece)
         fetch_wo = [fetch(b, b) for b in range(n_early)]
         for copy in fetch_wo:
@@ -82,7 +104,6 @@
             for j in range(heads_here):
                 head = src * heads_here + j
                 qs[n_rows * head : n_rows * (head + 1), :] = rotate(block[:, HD * j : HD * (j + 1)])
-        fetch_new.wait()
         fresh = new_ref[:, 0, :].astype(jnp.float32)
         for k in range(n_kv):
             ks[n_rows * k : n_rows * (k + 1), :] = rotate(fresh[:, HD * k : HD * (k + 1)])
@@ -92,8 +113,7 @@
         lane_group = lax.broadcasted_iota(jnp.int32, (1, n_heads), 1) // group
         slot = first_slot + lax.broadcasted_iota(jnp.int32, (block_len, n_heads), 0)
         own_kv = lax.broadcasted_iota(jnp.int32, (n_kv, n_heads), 0) == lane_group
-        for r in range(n_rows):
-            fetch_kv[r].wait()
+        def one_row(r):
             query = qs[pl.ds(r, n_heads, stride=n_rows), :].astype(jnp.bfloat16)
             keys = jnp.concatenate(
                 [kv_ref[r, 0, :, HD * k : HD * (k + 1)] for k in range(n_kv)], axis=0
@@ -125,7 +145,7 @@
             fresh_high = fresh_spread.astype(jnp.bfloat16)
             fresh_low = (fresh_spread - fresh_high.astype(jnp.float32)).astype(jnp.bfloat16)
             fresh_value = jnp.concatenate(
-                [new_ref[r : r + 1, 1, HD * k : HD * (k + 1)] for k in range(n_kv)], axis=0
+                [new_ref[pl.ds(r, 1), 1, HD * k : HD * (k + 1)] for k in range(n_kv)], axis=0
             )
             both = ((0,), (0,))
             summed = contract(high, values, both) + contract(low, values, both)
@@ -137,10 +157,17 @@
             pad = jnp.zeros((STAT_ROWS - len(parts), n_heads), jnp.float32)
             stats = jnp.concatenate([part.astype(jnp.float32) for part in parts] + [pad], axis=0)
             out_ref[r, n_heads : n_heads + STAT_ROWS, :] = stats.astype(jnp.bfloat16)
+
+        def some_rows(step, carry):
+            for u in range(ROW_UNROLL):
+                one_row(step * ROW_UNROLL + u)
+            return carry
+
+        lax.fori_loop(0, n_rows // ROW_UNROLL, some_rows, 0)
         for copy in fetch_wo:
             copy.wait()
 
-    in_vmem, in_hbm = pl.BlockSpec(memory_space=VMEM), pl.BlockSpec(memory_space=HBM)
+    in_vmem = pl.BlockSpec(memory_space=VMEM)
     return pl.pallas_call(
         body,
         out_shape=(
@@ -148,20 +175,18 @@
             pltpu.VMEM((n_early, wo.shape[0], piece), wo.dtype),
         ),
         in_specs=[pl.BlockSpec(memory_space=SMEM)]
-        + [in_vmem] * 3 + [in_hbm] * 2 + [in_vmem] * 2 + [in_hbm],
+        + [in_vmem] * 7 + [pl.BlockSpec(memory_space=HBM)],
         out_specs=(in_vmem, in_vmem),
         scratch_shapes=[
             pltpu.VMEM((n_rows * n_heads, HD), jnp.float32),
             pltpu.VMEM((n_rows * n_kv, HD), jnp.float32),
-            pltpu.VMEM(new_kv.shape, new_kv.dtype),
-            pltpu.VMEM(kv_codes.shape, kv_codes.dtype),
-            pltpu.SemaphoreType.DMA,
-            pltpu.SemaphoreType.DMA((n_rows,)),
             pltpu.SemaphoreType.DMA((n_early,)),
         ],
-        compiler_params=pltpu.CompilerParams(vmem_limit_bytes=12 * MIB),
+        compiler_params=pltpu.CompilerParams(vmem_limit_bytes=6 * MIB),
         name="attend",
-    )(scalars, gathered, cosine, sine, new_kv, kv_codes, key_scales, value_scales, wo)
+    )(
+        scalars, gathered, cosine, sine, new_kv, kv_codes, key_scales, value_scales, in_place(wo)
+    )
 
 
 def settle(main, stats, n_heads, stat_row, n_target, copies):
@@ -222,23 +247,26 @@
         fetch_wo = [fetch(n_early + b, b) for b in range(n_late)]
         for copy in fetch_wo:
             copy.start()
-        wide[...] = x_ref[...].astype(jnp.float32).reshape(n_all * heads_here, HD)
-        for j in range(heads_here):
-            pieces = [
-                wide[pl.ds(first * heads_here + j, n_rows, stride=heads_here * step), :]
-                for first, step in tiles
-            ]
-            packed[:, HD * j : HD * (j + 1)] = jnp.concatenate(pieces, axis=0).astype(jnp.bfloat16)
-        x = packed[...]
-        for b in range(n_block):
-            if b < n_early:
-                block = early_ref[b]
-            else:
-                fetch_wo[b - n_early].wait()
-                block = late[b - n_early]
-            share = jnp.dot(x, block, preferred_element_type=jnp.float32)
-            for s in range(len(tiles)):
-                out_ref[spot(b, s)] = share[s * n_rows : (s + 1) * n_rows].astype(jnp.bfloat16)
+
+        @pl.when(own_ref[0] >= 0)
+        def _():
+            wide[...] = x_ref[...].astype(jnp.float32).reshape(n_all * heads_here, HD)
+            for j in range(heads_here):
+                pieces = [
+                    wide[pl.ds(first * heads_here + j, n_rows, stride=heads_here * step), :]
+                    for first, step in tiles
+                ]
+                packed[:, HD * j : HD * (j + 1)] = jnp.concatenate(pieces, axis=0).astype(jnp.bfloat16)
+            x = packed[...]
+            for b in range(n_block):
+                if b < n_early:
+                    block = early_ref[b]
+                else:
+                    fetch_wo[b - n_early].wait()
+                    block = late[b - n_early]
+                share = jnp.dot(x, block, preferred_element_type=jnp.float32)
+                for s in range(len(tiles)):
+                    out_ref[spot(b, s)] = share[s * n_rows : (s + 1) * n_rows].astype(jnp.bfloat16)
 
     in_vmem = pl.BlockSpec(memory_space=VMEM)
     return pl.pallas_call(
@@ -256,7 +284,7 @@
         ],
         compiler_params=pltpu.CompilerParams(vmem_limit_bytes=24 * MIB),
         name="project",
-    )(own_share, rows, early, wo)
+    )(own_share, rows, early, in_place(wo))
 
 
 def finish(shares, scales, residual, n_head, n_share, spot):
@@ -317,13 +345,13 @@
     spread = jnp.repeat(jnp.swapaxes(kv_scales, 2, 3), n_heads // n_kv, axis=3)
     own_share = my_share.reshape(1).astype(jnp.int32)
     first_slot = (my_head * block_len).reshape(1).astype(jnp.int32)
-    scalars, own_share, gathered, cosine, sine, spread = lax.optimization_barrier(
-        (jnp.concatenate([lengths, first_slot, own_share]), own_share, gathered, cosine, sine, spread)
-    )
+    scalars = jnp.concatenate([lengths, first_slot, own_share])
+    new_staged, kv_staged = stage((new_kv, kv_codes))
     partial, early = attend(
-        scalars, gathered, cosine, sine, new_kv, kv_codes, spread[:, 0], spread[:, 1], wo_codes,
-        n_head // 2, piece,
-    )
+        scalars, gathered, cosine, sine, new_staged, kv_staged, spread[:, 0], spread[:, 1], wo_codes,
+        EARLY_EIGHTHS * n_head // 8, piece,
+    )
+    own_share, partial = lax.optimization_barrier((own_share, partial))
 
     cuts = max(1, n_head // n_rows)
     depth = HD // cuts

time: 69.8 us -> 63.2 us (0.905)
  waiting for transfers between devices: 7.33 us -> 4.7 us
  Pallas kernels: 12.4 us -> 10.4 us
  local copies, waits for them, and re-layouts: 4.7 us -> 2.8 us
    all_to_all x1, waiting for transfers between devices: 7.33 us -> 4.7 us  [exchange(): return lax.all_to_all(block, axes, split_axis=0, concat_axis=0, tiled=True)]
    pallas_call x1, Pallas kernels: 6.02 us -> 3.48 us  [attend(): pl.pallas_call(body, out_shape=(jax.ShapeDtypeStruct((n_rows, n_heads + S...]
    unnamed x8 -> x6, local copies, waits for them, and re-layouts: 1.98 us -> 0.35 us
    pallas_call x0 -> x1, Pallas kernels: none -> 1.27 us  [stage(): pl.pallas_call(body, out_shape=tuple((pltpu.VMEM(a.shape, a.dtype) for a...]
    pallas_call x1, Pallas kernels: 5.42 us -> 4.63 us  [project(): pl.pallas_call(body, out_shape=jax.ShapeDtypeStruct((n_block * len(tiles)...]
  transfers between devices with their start and end apart: 1 -> 1, of which waited for: 1 -> 1; matrix products, arithmetic and copies ran while one was open for 2% -> 5% of each run, Pallas kernels for 0% -> 2%
where the time goes in v4:
time: 63.2 us; the launch traced here: 62.7 us
  blocking collectives  35.9 us (57%)
  Pallas kernels  10.4 us (16%)
  starting transfers between devices  7.28 us (12%)
  waiting for transfers between devices  4.7 us (7%)
  local copies, waits for them, and re-layouts  2.8 us (4%)
  other arithmetic  1.59 us (3%)
    all_to_all x3, blocking collectives, exchange(): return lax.all_to_all(block, axes, split_axis=0, concat_axis=0, tiled=True)  35.9 us
    all_to_all x1, starting transfers between devices, exchange(): return lax.all_to_all(block, axes, split_axis=0, concat_axis=0, tiled=True)  7.28 us
    all_to_all x1, waiting for transfers between devices, exchange(): return lax.all_to_all(block, axes, split_axis=0, concat_axis=0, tiled=True)  4.7 us
    pallas_call x1, Pallas kernels, project(): pl.pallas_call(body, out_shape=jax.ShapeDtypeStruct((n_block * len(tiles)...  4.63 us
    pallas_call x1, Pallas kernels, attend(): pl.pallas_call(body, out_shape=(jax.ShapeDtypeStruct((n_rows, n_heads + S...  3.48 us
    broadcast_in_dim x1, local copies, waits for them, and re-layouts, on_device(): jnp.broadcast_to(queries, (n_head, n_rows, width))  1.47 us
    pallas_call x1, Pallas kernels, stage(): pl.pallas_call(body, out_shape=tuple((pltpu.VMEM(a.shape, a.dtype) for a...  1.27 us
  transfers between devices with their start and end apart: 1, of which 1 were waited for; matrix products, arithmetic and copies ran while one was open for 5% of the time, Pallas kernels for 2%

profile of v4, /device:TPU:0, one launch (start us, length us, event | category | flops | bytes accessed | tf_op | source)
XLA Modules:
  0.0 62.7 jit_solution(9757167625489985892)
XLA Ops:
  0.0 1.5 %broadcast_in_dim.8 = bf16[8,8,2048]{2,1,0:T(8,128)(2,1)} broadcast(bf16[8,2048]{1,0:T(8,128)(2,1)} %param.9), dimensions={1,2} | broadcast | bytes 294912 | tf_op jit(solution)/shard_map/broadcast_in_dim | solution.py:343
  1.5 7.3 %all-to-all-start = ((bf16[8,8,2048]{2,1,0:T(8,128)(2,1)}), bf16[8,8,2048]{2,1,0:T(8,128)(2,1)S(1)}, u32[]{:S(2)}, u32[]{:S(2)}) async-start(bf16[8,8,2048]{2,1,0:T(8,128)(2,1)} %broadcast_in_dim.8), calls=%async_computation | async-start | bytes 524288 | tf_op jit(solution)/shard_map/all_to_all | solution.py:314
  8.8 0.9 %broadcast_in_dim.9 = f32[8,2,32,8,16]{2,4,3,1,0:T(8,128)S(1)} broadcast(f32[8,2,32,8]{2,3,1,0:T(8,128)} %bitcast.11), dimensions={0,1,2,3} | broadcast | bytes 278528 | tf_op jit(solution)/shard_map/broadcast_in_dim | solution.py:345
  9.7 0.1 fusion.1
  9.8 0.7 %convert_element_type.3 = f32[8]{0:T(128)S(1)} convert(s32[8]{0:T(128)} %param.11) | non-fusion elementwise | flops 8 | bytes 64 | tf_op jit(solution)/shard_map/convert_element_type | solution.py:40
  10.4 0.2 copy.14
  10.6 0.2 copy.13
  10.8 1.3 %stage.1 = (bf16[8,2,1024]{2,1,0:T(2,128)(2,1)S(1)}, bf16[8,2,32,1024]{3,2,1,0:T(8,128)(2,1)S(1)}) custom-call(bf16[8,2,1024]{2,1,0:T(2,128)(2,1)} %refs_0_.1, bf16[8,2,32,1024]{3,2,1,0:T(8,128)(2,1)} %refs_1_.1), custom_call_target="tpu_custom_call" | custom-call | tf_op jit(solution)/shard_map/stage/pallas_call | solution.py:58
  12.1 0.7 %pad_add_fusion.s_ref = s32[10]{0:T(128)S(1)} fusion(s32[1]{0:T(128)} %bitcast.own_ref, s32[1]{0:T(128)} %bitcast.1, s32[8]{0:T(128)} %param.12), kind=kLoop, calls=%fused_computation.5 | loop fusion | flops 20 | bytes 80 | tf_op jit(solution)/shard_map/concatenate | solution.py:348
  12.8 0.1 fusion
  12.9 0.1 pad_maximum_fusion
  13.0 4.7 %all-to-all-done.q_ref = bf16[8,8,2048]{2,1,0:T(8,128)(2,1)S(1)} async-done(((bf16[8,8,2048]{2,1,0:T(8,128)(2,1)}), bf16[8,8,2048]{2,1,0:T(8,128)(2,1)S(1)}, u32[]{:S(2)}, u32[]{:S(2)}) %all-to-all-start) | async-done | bytes 262176 | tf_op jit(solution)/shard_map/all_to_all | solution.py:314
  17.7 0.0 copy-start
  17.7 0.0 copy-start.1
  17.7 3.5 %attend.1 = (bf16[8,136,128]{2,1,0:T(8,128)(2,1)S(1)}, bf16[3,2048,512]{2,1,0:T(8,128)(2,1)S(1)}) custom-call(s32[10]{0:T(128)S(1)} %pad_add_fusion.s_ref, bf16[8,8,2048]{2,1,0:T(8,128)(2,1)S(1)} %all-to-all-done.q_ref, f32[8,128]{1,0:T(8,128)S(1)} %get-tuple-element.22.cos_ref, f32[8,128]{1,0:T(8,128)S(1)} %get-tuple-element.23.sin_ref, ...), custom_call_target="tpu_custom_call" | custom-call | tf_op jit(solution)/shard_map/attend/pallas_call | solution.py:171
  21.2 13.1 %all_to_all.20.main_ref.stat_ref = bf16[8,136,128]{2,1,0:T(8,128)(2,1)S(1)} all-to-all(bf16[8,136,128]{2,1,0:T(8,128)(2,1)S(1)} %get-tuple-element.15), channel_id=1, replica_groups=mesh['group'=2,'head'=8,'dp'=2] {'head'}, dimensions={0} | all-to-all | bytes 557056 | tf_op jit(solution)/shard_map/all_to_all | solution.py:314
  34.3 0.3 settle.1
  34.6 10.8 %all_to_all.21.x_ref = bf16[32,16,128]{2,1,0:T(8,128)(2,1)S(1)} all-to-all(bf16[32,16,128]{2,1,0:T(8,128)(2,1)S(1)} %settle.1), channel_id=1, replica_groups=mesh['group'=2,'head'=8,'dp'=2] {'group','head','dp'}, dimensions={0} | all-to-all | bytes 262144 | tf_op jit(solution)/shard_map/all_to_all | solution.py:314
  45.5 4.6 %project.1 = bf16[32,8,512]{2,1,0:T(8,128)(2,1)S(1)} custom-call(s32[1]{0:T(128)} %bitcast.own_ref, bf16[32,16,128]{2,1,0:T(8,128)(2,1)S(1)} %all_to_all.21.x_ref, bf16[3,2048,512]{2,1,0:T(8,128)(2,1)S(1)} %get-tuple-element.16.early_ref, bf16[2048,16384]{1,0:T(8,128)(2,1)} %wo_ref.3), custom_call_target="tpu_custom_call" | custom-call | tf_op jit(solution)/shard_map/project/pallas_call | solution.py:272
  50.1 12.0 %all_to_all.22.share_ref = bf16[32,8,512]{2,1,0:T(8,128)(2,1)S(1)} all-to-all(bf16[32,8,512]{2,1,0:T(8,128)(2,1)S(1)} %project.1), channel_id=1, replica_groups=mesh['group'=2,'head'=8,'dp'=2] {'group','head','dp'}, dimensions={0} | all-to-all | bytes 524288 | tf_op jit(solution)/shard_map/all_to_all | solution.py:314
  62.1 0.0 copy-done
  62.1 0.0 copy-done.1
  62.1 0.7 %finish.1 = bf16[8,2048]{1,0:T(8,128)(2,1)} custom-call(bf16[32,8,512]{2,1,0:T(8,128)(2,1)S(1)} %all_to_all.22.share_ref, f32[1,2048]{1,0:T(1,128)S(1)} %bitcast.9, bf16[8,2048]{1,0:T(8,128)(2,1)S(1)} %copy-done), custom_call_target="tpu_custom_call" | custom-call | tf_op jit(solution)/shard_map/finish/pallas_call | solution.py:303
  (1 shorter events, 0.0 us)
Async XLA Ops:
  1.5 16.2 %all-to-all-start = ((bf16[8,8,2048]{2,1,0:T(8,128)(2,1)}), bf16[8,8,2048]{2,1,0:T(8,128)(2,1)S(1)}, u32[]{:S(2)}, u32[]{:S(2)}) async-start(bf16[8,8,2048]{2,1,0:T(8,128)(2,1)} %broadcast_in_dim.8), calls=%async_computation | async-start | bytes 524288 | tf_op jit(solution)/shard_map/all_to_all | solution.py:314
  17.7 44.4 %copy-start = (bf16[8,2048]{1,0:T(8,128)(2,1)S(1)}, bf16[8,2048]{1,0:T(8,128)(2,1)}, u32[]{:S(2)}) copy-start(bf16[8,2048]{1,0:T(8,128)(2,1)} %res_ref.1) | copy-start | bytes 98308
  17.7 44.4 %copy-start.1 = (f32[2048]{0:T(1024)S(1)}, f32[2048]{0:T(1024)}, u32[]{:S(2)}) copy-start(f32[2048]{0:T(1024)} %param.16) | copy-start | bytes 24580

commit v5 on v4

--- a/solution.py
+++ b/solution.py
@@ -6,11 +6,13 @@
 from jax.experimental.pallas import tpu as pltpu
 from jax.sharding import PartitionSpec as P
 
+
 HD = 128
 ROPE_BASE = 500000.0
 NEG_FILL = -1e30
 STAT_ROWS = 8
-ROW_UNROLL = 4
+SIDE_ROWS = 8
+ROW_UNROLL = 2
 EARLY_EIGHTHS = 3
 MIB = 1 << 20
 VMEM = pltpu.MemorySpace.VMEM
@@ -43,11 +45,62 @@
     return jnp.concatenate([cosine, cosine], -1), jnp.concatenate([-sine, sine], -1)
 
 
-def stage(arrays):
-    def body(*refs):
-        count = len(arrays)
+def prepare(own_half, queries, kv_codes, kv_scales, count):
+    half = queries.shape[0] // 2
+    width = queries.shape[1]
+
+    def body(own_ref, q_hbm, kv_hbm, sc_hbm, out_ref, k_ref, v_ref, sc_ref, whole, parts, sem):
+        other = (1 - own_ref[0]) * half
+        loads = [
+            pltpu.make_async_copy(q_hbm, whole, sem.at[0]),
+            pltpu.make_async_copy(kv_hbm.at[pl.ds(other, half), 0], k_ref, sem.at[1]),
+            pltpu.make_async_copy(kv_hbm.at[pl.ds(other, half), 1], v_ref, sem.at[2]),
+            pltpu.make_async_copy(sc_hbm.at[pl.ds(other, half)], sc_ref, sem.at[3]),
+        ]
+        for copy in loads:
+            copy.start()
+        loads[0].wait()
+        for p in range(2):
+            parts[p] = whole[p * half : (p + 1) * half, :]
+        sends = [
+            pltpu.make_async_copy(parts.at[n % 2], out_ref.at[n], sem.at[4 + n])
+            for n in range(count)
+        ]
+        for copy in sends:
+            copy.start()
+        for copy in loads[1:] + sends:
+            copy.wait()
+
+    in_hbm, in_vmem = pl.BlockSpec(memory_space=HBM), pl.BlockSpec(memory_space=VMEM)
+    return pl.pallas_call(
+        body,
+        out_shape=(
+            pltpu.HBM((count, half, width), queries.dtype),
+            pltpu.VMEM((half,) + kv_codes.shape[2:], kv_codes.dtype),
+            pltpu.VMEM((half,) + kv_codes.shape[2:], kv_codes.dtype),
+            pltpu.VMEM((half,) + kv_scales.shape[1:], kv_scales.dtype),
+        ),
+        in_specs=[pl.BlockSpec(memory_space=SMEM)] + [in_hbm] * 3,
+        out_specs=(in_hbm, in_vmem, in_vmem, in_vmem),
+        scratch_shapes=[
+            pltpu.VMEM(queries.shape, queries.dtype),
+            pltpu.VMEM((2, half, width), queries.dtype),
+            pltpu.SemaphoreType.DMA((4 + count,)),
+        ],
+        compiler_params=pltpu.CompilerParams(vmem_limit_bytes=MIB // 2),
+        name="prepare",
+    )(own_half, in_place(queries), in_place(kv_codes), in_place(kv_scales))
+
+
+def stage(own_half, arrays):
+    half = arrays[0].shape[0] // 2
+    count = len(arrays)
+
+    def body(own_ref, *refs):
+        first = own_ref[0] * half
         copies = [
-            pltpu.make_async_copy(refs[n], refs[count + n], refs[-1].at[n]) for n in range(count)
+            pltpu.make_async_copy(refs[n].at[pl.ds(first, half)], refs[count + n], refs[-1].at[n])
+            for n in range(count)
         ]
         for copy in copies:
             copy.start()
@@ -57,13 +110,13 @@
     in_hbm, in_vmem = pl.BlockSpec(memory_space=HBM), pl.BlockSpec(memory_space=VMEM)
     return pl.pallas_call(
         body,
-        out_shape=tuple(pltpu.VMEM(a.shape, a.dtype) for a in arrays),
-        in_specs=[in_hbm] * len(arrays),
-        out_specs=(in_vmem,) * len(arrays),
-        scratch_shapes=[pltpu.SemaphoreType.DMA((len(arrays),))],
+        out_shape=tuple(pltpu.VMEM((half,) + a.shape[1:], a.dtype) for a in arrays),
+        in_specs=[pl.BlockSpec(memory_space=SMEM)] + [in_hbm] * count,
+        out_specs=(in_vmem,) * count,
+        scratch_shapes=[pltpu.SemaphoreType.DMA((count,))],
         compiler_params=pltpu.CompilerParams(vmem_limit_bytes=MIB // 4),
         name="stage",
-    )(*[in_place(a) for a in arrays])
+    )(own_half, *[in_place(a) for a in arrays])
 
 
 def weight_fetch(wo_ref, out_ref, sem, share, n_block, piece):
@@ -75,22 +128,23 @@
     return fetch
 
 
-def attend(
-    scalars, gathered, cosine, sine, new_kv, kv_codes, key_scales, value_scales, wo, n_early, piece
+def score(
+    scalars, gathered, cosine, sine, new_kv, own_kv, other_keys, own_scales, other_scales, wo,
+    n_early, piece,
 ):
     n_src, n_rows, width = gathered.shape
     heads_here = width // HD
     n_heads = n_src * heads_here
-    block_len = kv_codes.shape[2]
-    n_kv = kv_codes.shape[3] // HD
+    block_len = own_kv.shape[2]
+    n_kv = own_kv.shape[3] // HD
     group = n_heads // n_kv
     score_scale = HD ** (-0.5)
 
     def body(
-        s_ref, q_ref, cos_ref, sin_ref, new_ref, kv_ref, ks_ref, vs_ref, wo_ref, out_ref, early_ref,
-        qs, ks, wo_sem,
+        s_ref, q_ref, cos_ref, sin_ref, new_ref, own_ref, other_ref, own_sc, other_sc, wo_ref,
+        weight_ref, side_ref, early_ref, qs, ks, wo_sem,
     ):
-        fetch = weight_fetch(wo_ref, early_ref, wo_sem, s_ref[n_rows + 1], n_src, piece)
+        fetch = weight_fetch(wo_ref, early_ref, wo_sem, s_ref[n_rows + 3], n_src, piece)
         fetch_wo = [fetch(b, b) for b in range(n_early)]
         for copy in fetch_wo:
             copy.start()
@@ -108,46 +162,120 @@
         for k in range(n_kv):
             ks[n_rows * k : n_rows * (k + 1), :] = rotate(fresh[:, HD * k : HD * (k + 1)])
 
-        first_slot = s_ref[n_rows]
-        is_first = first_slot == 0
+        is_first = s_ref[n_rows + 2] == 0
         lane_group = lax.broadcasted_iota(jnp.int32, (1, n_heads), 1) // group
-        slot = first_slot + lax.broadcasted_iota(jnp.int32, (block_len, n_heads), 0)
-        own_kv = lax.broadcasted_iota(jnp.int32, (n_kv, n_heads), 0) == lane_group
+        place = lax.broadcasted_iota(jnp.int32, (block_len, n_heads), 0)
+        slot = jnp.concatenate([s_ref[n_rows] + place, s_ref[n_rows + 1] + place], axis=0)
+        owner = lax.broadcasted_iota(jnp.int32, (n_kv, n_heads), 0) == lane_group
+        one_hot = owner.astype(jnp.float32)
+        both = ((0,), (0,))
+
+        def spread(kind, r):
+            parts = [
+                lax.dot_general(
+                    ref[r, kind], one_hot, (both, ((), ())), precision=lax.Precision.HIGHEST,
+                    preferred_element_type=jnp.float32,
+                )
+                for ref in (own_sc, other_sc)
+            ]
+            return jnp.concatenate(parts, axis=0)
+
+        def keys_of(r):
+            parts = [own_ref[r, 0, :, HD * k : HD * (k + 1)] for k in range(n_kv)]
+            parts += [other_ref[r, :, HD * k : HD * (k + 1)] for k in range(n_kv)]
+            return jnp.concatenate(parts, axis=0)
+
         def one_row(r):
             query = qs[pl.ds(r, n_heads, stride=n_rows), :].astype(jnp.bfloat16)
-            keys = jnp.concatenate(
-                [kv_ref[r, 0, :, HD * k : HD * (k + 1)] for k in range(n_kv)], axis=0
-            )
-            values = jnp.concatenate(
-                [kv_ref[r, 1, :, HD * k : HD * (k + 1)] for k in range(n_kv)], axis=0
-            )
-            raw = contract(keys, query, ((1,), (1,)))
-            raw_own = jnp.zeros((block_len, n_heads), jnp.float32)
-            for k in range(n_kv):
-                raw_own = jnp.where(lane_group == k, raw[block_len * k : block_len * (k + 1)], raw_own)
+            raw = contract(keys_of(r), query, ((1,), (1,)))
+            halves = []
+            for base in (0, n_kv):
+                picked = jnp.zeros((block_len, n_heads), jnp.float32)
+                for k in range(n_kv):
+                    first = block_len * (base + k)
+                    picked = jnp.where(lane_group == k, raw[first : first + block_len], picked)
+                halves.append(picked)
+            raw_own = jnp.concatenate(halves, axis=0)
             is_valid = slot < s_ref[r]
-            scores = jnp.where(is_valid, raw_own * ks_ref[r] * score_scale, NEG_FILL)
+            scores = jnp.where(is_valid, raw_own * spread(0, r) * score_scale, NEG_FILL)
             fresh_key = ks[pl.ds(r, n_kv, stride=n_rows), :].astype(jnp.bfloat16)
             fresh_raw = contract(fresh_key, query, ((1,), (1,)))
-            fresh_score = jnp.sum(jnp.where(own_kv, fresh_raw, 0.0), axis=0, keepdims=True) * score_scale
+            fresh_score = jnp.sum(jnp.where(owner, fresh_raw, 0.0), axis=0, keepdims=True) * score_scale
             fresh_score = jnp.where(is_first, fresh_score, NEG_FILL)
             peak = jnp.maximum(jnp.max(scores, axis=0, keepdims=True), fresh_score)
             weights = jnp.where(is_valid, jnp.exp(scores - peak), 0.0)
             fresh_weight = jnp.where(is_first, jnp.exp(fresh_score - peak), 0.0)
             total = jnp.sum(weights, axis=0, keepdims=True) + fresh_weight
-            scaled = weights * vs_ref[r]
-            spread = jnp.concatenate(
-                [jnp.where(lane_group == k, scaled, 0.0) for k in range(n_kv)], axis=0
+            weight_ref[r] = weights * spread(1, r)
+            pad = jnp.zeros((SIDE_ROWS - 3, n_heads), jnp.float32)
+            side_ref[r] = jnp.concatenate([peak, total, fresh_weight, pad], axis=0)
+
+        def some_rows(step, carry):
+            for u in range(ROW_UNROLL):
+                one_row(step * ROW_UNROLL + u)
+            return carry
+
+        lax.fori_loop(0, n_rows // ROW_UNROLL, some_rows, 0)
+        for copy in fetch_wo:
+            copy.wait()
+
+    in_vmem = pl.BlockSpec(memory_space=VMEM)
+    return pl.pallas_call(
+        body,
+        out_shape=(
+            pltpu.VMEM((n_rows, 2 * block_len, n_heads), jnp.float32),
+            pltpu.VMEM((n_rows, SIDE_ROWS, n_heads), jnp.float32),
+            pltpu.VMEM((n_early, wo.shape[0], piece), wo.dtype),
+        ),
+        in_specs=[pl.BlockSpec(memory_space=SMEM)]
+        + [in_vmem] * 8 + [pl.BlockSpec(memory_space=HBM)],
+        out_specs=(in_vmem,) * 3,
+        scratch_shapes=[
+            pltpu.VMEM((n_rows * n_heads, HD), jnp.float32),
+            pltpu.VMEM((n_rows * n_kv, HD), jnp.float32),
+            pltpu.SemaphoreType.DMA((n_early,)),
+        ],
+        compiler_params=pltpu.CompilerParams(vmem_limit_bytes=6 * MIB),
+        name="score",
+    )(
+        scalars, gathered, cosine, sine, new_kv, own_kv, other_keys, own_scales, other_scales,
+        in_place(wo),
+    )
+
+
+def blend(weights, side, new_kv, own_kv, other_values):
+    n_rows, _, n_heads = weights.shape
+    block_len = own_kv.shape[2]
+    n_kv = own_kv.shape[3] // HD
+    group = n_heads // n_kv
+
+    def body(weight_ref, side_ref, new_ref, own_ref, other_ref, out_ref):
+        lane_group = lax.broadcasted_iota(jnp.int32, (1, n_heads), 1) // group
+        owner = lax.broadcasted_iota(jnp.int32, (n_kv, n_heads), 0) == lane_group
+        both = ((0,), (0,))
+
+        def one_row(r):
+            scaled = weight_ref[r]
+            wide = jnp.concatenate(
+                [
+                    jnp.where(lane_group == k, scaled[first : first + block_len], 0.0)
+                    for first in (0, block_len)
+                    for k in range(n_kv)
+                ],
+                axis=0,
             )
-            high = spread.astype(jnp.bfloat16)
-            low = (spread - high.astype(jnp.float32)).astype(jnp.bfloat16)
-            fresh_spread = jnp.where(own_kv, fresh_weight, 0.0)
+            high = wide.astype(jnp.bfloat16)
+            low = (wide - high.astype(jnp.float32)).astype(jnp.bfloat16)
+            peak, total, fresh_weight = side_ref[r, 0:1], side_ref[r, 1:2], side_ref[r, 2:3]
+            fresh_spread = jnp.where(owner, fresh_weight, 0.0)
             fresh_high = fresh_spread.astype(jnp.bfloat16)
             fresh_low = (fresh_spread - fresh_high.astype(jnp.float32)).astype(jnp.bfloat16)
             fresh_value = jnp.concatenate(
                 [new_ref[pl.ds(r, 1), 1, HD * k : HD * (k + 1)] for k in range(n_kv)], axis=0
             )
-            both = ((0,), (0,))
+            values = [own_ref[r, 1, :, HD * k : HD * (k + 1)] for k in range(n_kv)]
+            values += [other_ref[r, :, HD * k : HD * (k + 1)] for k in range(n_kv)]
+            values = jnp.concatenate(values, axis=0)
             summed = contract(high, values, both) + contract(low, values, both)
             summed = summed + (
                 contract(fresh_high, fresh_value, both) + contract(fresh_low, fresh_value, both)
@@ -158,35 +286,17 @@
             stats = jnp.concatenate([part.astype(jnp.float32) for part in parts] + [pad], axis=0)
             out_ref[r, n_heads : n_heads + STAT_ROWS, :] = stats.astype(jnp.bfloat16)
 
-        def some_rows(step, carry):
-            for u in range(ROW_UNROLL):
-                one_row(step * ROW_UNROLL + u)
-            return carry
-
-        lax.fori_loop(0, n_rows // ROW_UNROLL, some_rows, 0)
-        for copy in fetch_wo:
-            copy.wait()
-
-    in_vmem = pl.BlockSpec(memory_space=VMEM)
-    return pl.pallas_call(
-        body,
-        out_shape=(
-            jax.ShapeDtypeStruct((n_rows, n_heads + STAT_ROWS, HD), jnp.bfloat16),
-            pltpu.VMEM((n_early, wo.shape[0], piece), wo.dtype),
-        ),
-        in_specs=[pl.BlockSpec(memory_space=SMEM)]
-        + [in_vmem] * 7 + [pl.BlockSpec(memory_space=HBM)],
-        out_specs=(in_vmem, in_vmem),
-        scratch_shapes=[
-            pltpu.VMEM((n_rows * n_heads, HD), jnp.float32),
-            pltpu.VMEM((n_rows * n_kv, HD), jnp.float32),
-            pltpu.SemaphoreType.DMA((n_early,)),
-        ],
+        for r in range(n_rows):
+            one_row(r)
+
+    return pl.pallas_call(
+        body,
+        out_shape=jax.ShapeDtypeStruct((n_rows, n_heads + STAT_ROWS, HD), jnp.bfloat16),
+        in_specs=[pl.BlockSpec(memory_space=VMEM)] * 5,
+        out_specs=pl.BlockSpec(memory_space=VMEM),
         compiler_params=pltpu.CompilerParams(vmem_limit_bytes=6 * MIB),
-        name="attend",
-    )(
-        scalars, gathered, cosine, sine, new_kv, kv_codes, key_scales, value_scales, in_place(wo)
-    )
+        name="blend",
+    )(weights, side, new_kv, own_kv, other_values)
 
 
 def settle(main, stats, n_heads, stat_row, n_target, copies):
@@ -290,12 +400,19 @@
 def finish(shares, scales, residual, n_head, n_share, spot):
     piece = shares.shape[2]
 
-    def body(share_ref, scale_ref, res_ref, out_ref):
+    n_rows = shares.shape[1]
+
+    def body(share_ref, scale_ref, res_ref, out_ref, held):
         for s in range(n_share):
             total = share_ref[spot(0, s)].astype(jnp.float32)
             for h in range(1, n_head):
                 total = total + share_ref[spot(h, s)].astype(jnp.float32)
-            cols = slice(s * piece, (s + 1) * piece)
+            for c in range(piece // HD):
+                held[s * (piece // HD) + c] = total[:, HD * c : HD * (c + 1)]
+        for c in range(n_share * piece // HD):
+            cols = slice(HD * c, HD * (c + 1))
+            ordered = [held[c, pl.ds(p, n_rows // 2, stride=2), :] for p in range(2)]
+            total = jnp.concatenate(ordered, axis=0)
             out_ref[:, cols] = (
                 res_ref[:, cols].astype(jnp.float32) + total * scale_ref[:, cols]
             ).astype(jnp.bfloat16)
@@ -305,13 +422,16 @@
         out_shape=jax.ShapeDtypeStruct(residual.shape, jnp.bfloat16),
         in_specs=[pl.BlockSpec(memory_space=VMEM)] * 3,
         out_specs=pl.BlockSpec(memory_space=VMEM),
+        scratch_shapes=[pltpu.VMEM((n_share * piece // HD, n_rows, HD), jnp.float32)],
         compiler_params=pltpu.CompilerParams(vmem_limit_bytes=16 * MIB),
         name="finish",
     )(shares, scales, residual)
 
 
-def exchange(block, axes):
-    return lax.all_to_all(block, axes, split_axis=0, concat_axis=0, tiled=True)
+def exchange(block, axes, groups=None):
+    return lax.all_to_all(
+        block, axes, split_axis=0, concat_axis=0, tiled=True, axis_index_groups=groups
+    )
 
 
 def on_device(
@@ -323,7 +443,6 @@
     n_rows, width = queries.shape
     heads_here = width // HD
     n_heads = heads_here * n_head
-    n_kv = new_kv.shape[2] // HD
     block_len = kv_codes.shape[2]
     own_cols = wo_codes.shape[1] // n_head
     n_group = lax.axis_size("group")
@@ -340,39 +459,59 @@
     def spot(head, share):
         return (share // n_dp * n_head + head) * n_dp + share % n_dp
 
-    gathered = exchange(jnp.broadcast_to(queries, (n_head, n_rows, width)), "head")
-    cosine, sine = rotary_tables(positions)
-    spread = jnp.repeat(jnp.swapaxes(kv_scales, 2, 3), n_heads // n_kv, axis=3)
+    half = n_rows // 2
+    n_line = n_head // 2
+    my_line = my_head // 2
+    parity = (my_head % 2).astype(jnp.int32)
+    pairs = [(i, i ^ 1) for i in range(n_head)]
+    lines = [list(range(p, n_head, 2)) for p in range(2)]
+
+    def rows_of(array, side):
+        return lax.dynamic_slice_in_dim(array, side * half, half, axis=0)
+
+    own_half = parity.reshape(1)
+    messages, keys_out, values_out, scales_out = prepare(
+        own_half, queries, kv_codes, kv_scales, n_head
+    )
+    other_keys = lax.ppermute(keys_out, "head", pairs)
+    other_scales = lax.ppermute(scales_out, "head", pairs)
+    gathered = exchange(messages, "head")
+    other_values = lax.ppermute(values_out, "head", pairs)
+    cosine, sine = rotary_tables(rows_of(positions, parity))
     own_share = my_share.reshape(1).astype(jnp.int32)
-    first_slot = (my_head * block_len).reshape(1).astype(jnp.int32)
-    scalars = jnp.concatenate([lengths, first_slot, own_share])
-    new_staged, kv_staged = stage((new_kv, kv_codes))
-    partial, early = attend(
-        scalars, gathered, cosine, sine, new_staged, kv_staged, spread[:, 0], spread[:, 1], wo_codes,
-        EARLY_EIGHTHS * n_head // 8, piece,
-    )
+    slots = [my_head * block_len, (my_head ^ 1) * block_len, my_line]
+    slots = jnp.stack(slots).astype(jnp.int32)
+    scalars = jnp.concatenate([rows_of(lengths, parity), slots, own_share])
+    new_staged, kv_staged, scales_staged = stage(
+        own_half, (new_kv, kv_codes, kv_scales)
+    )
+    weights, side, early = score(
+        scalars, gathered, cosine, sine, new_staged, kv_staged, other_keys, scales_staged,
+        other_scales, wo_codes, EARLY_EIGHTHS * n_head // 8, piece,
+    )
+    partial = blend(weights, side, new_staged, kv_staged, other_values)
     own_share, partial = lax.optimization_barrier((own_share, partial))
 
-    cuts = max(1, n_head // n_rows)
+    cuts = max(1, n_line // half)
     depth = HD // cuts
     if cuts == 1:
-        main = exchange(partial, "head")
+        main = exchange(partial, "head", lines)
         stats, stat_row = main, n_heads
     else:
-        values = partial[:, :n_heads].reshape(n_rows, n_heads, cuts, depth).swapaxes(1, 2)
-        stats = partial[:, n_heads:].reshape(n_rows, 1, STAT_ROWS * cuts, depth)
-        stats = jnp.broadcast_to(stats, (n_rows, cuts) + stats.shape[2:])
+        values = partial[:, :n_heads].reshape(half, n_heads, cuts, depth).swapaxes(1, 2)
+        stats = partial[:, n_heads:].reshape(half, 1, STAT_ROWS * cuts, depth)
+        stats = jnp.broadcast_to(stats, (half, cuts) + stats.shape[2:])
         message = jnp.concatenate([values, stats], axis=2)
-        received = exchange(message.reshape((n_head,) + message.shape[2:]), "head")
+        received = exchange(message.reshape((n_line,) + message.shape[2:]), "head", lines)
         main, stat_row = received[:, :n_heads], 0
-        stats = received[:, n_heads:].reshape(n_head, STAT_ROWS, HD)
+        stats = received[:, n_heads:].reshape(n_line, STAT_ROWS, HD)
     copies = settle(
         main, stats, n_heads, stat_row, n_head, lambda h: [spot(h, s) for s in range(n_share)]
     )
     rows = exchange(copies, axes)
     if cuts > 1:
-        rows = rows.reshape(n_group, n_rows, cuts, n_dp, heads_here, depth)
-        rows = rows.transpose(0, 1, 3, 4, 2, 5).reshape(n_rows * n_share, heads_here, HD)
+        rows = rows.reshape(n_group, half, cuts, 2, n_dp, heads_here, depth)
+        rows = rows.transpose(0, 1, 3, 4, 5, 2, 6).reshape(n_rows * n_share, heads_here, HD)
     tiles = [(s // n_dp * n_rows * n_dp + s % n_dp, n_dp) for s in range(n_share)]
     shares = exchange(project(own_share, rows, early, wo_codes, n_head, tiles, spot), axes)
     return finish(shares, wo_scales.reshape(1, own_cols), residual, n_head, n_share, spot)

time: 63.2 us -> 64.5 us (1.021)
  starting transfers between devices: 7.28 us -> 11.3 us
  blocking collectives: 35.9 us -> 32.8 us
  local copies, waits for them, and re-layouts: 2.8 us -> 0.82 us
  Pallas kernels: 10.4 us -> 12.2 us
  waiting for transfers between devices: 4.7 us -> 5.81 us
  other arithmetic: 1.59 us -> 0.93 us
    ppermute x0 -> x3, waiting for transfers between devices: none -> 5.28 us  [the longest x1 4.27 us: on_device(): other_keys = lax.ppermute(keys_out, 'head', pairs)]
    all_to_all x1, waiting for transfers between devices: 4.7 us -> 0.53 us  [exchange(): lax.all_to_all(block, axes, split_axis=0, concat_axis=0, tiled=True, axis...]
    ppermute x0 -> x3, starting transfers between devices: none -> 4.05 us  [the longest x1 2.02 us: on_device(): other_scales = lax.ppermute(scales_out, 'head', pairs)]
    all_to_all x3, blocking collectives: 35.9 us -> 32.8 us  [exchange(): lax.all_to_all(block, axes, split_axis=0, concat_axis=0, tiled=True, axis...]
    broadcast_in_dim x2 -> x0, local copies, waits for them, and re-layouts: 2.38 us -> none  [the longest x1 1.47 us: on_device(): jnp.broadcast_to(queries, (n_head, n_rows, width))]
    pallas_call x2 -> x4, Pallas kernels: 4.75 us -> 6.68 us  [the longest x1 3.51 us: score(): pl.pallas_call(body, out_shape=(pltpu.VMEM((n_rows, 2 * block_len, n_head...]
    dynamic_slice x0 -> x1, local copies, waits for them, and re-layouts: none -> 0.73 us  [rows_of(): return lax.dynamic_slice_in_dim(array, side * half, half, axis=0)]
    concatenate x1 -> x0, other arithmetic: 0.73 us -> none  [on_device(): scalars = jnp.concatenate([lengths, first_slot, own_share])]
  transfers between devices with their start and end apart: 1 -> 4, of which waited for: 1 -> 3; matrix products, arithmetic and copies ran while one was open for 5% -> 3% of each run, Pallas kernels for 2% -> 7%
where the time goes in v5:
time: 64.5 us; the launch traced here: 64 us
  blocking collectives  32.8 us (51%)
  Pallas kernels  12.2 us (19%)
  starting transfers between devices  11.3 us (18%)
  waiting for transfers between devices  5.81 us (9%)
  other arithmetic  0.93 us (1%)
  local copies, waits for them, and re-layouts  0.82 us (1%)
    all_to_all x3, blocking collectives, exchange(): lax.all_to_all(block, axes, split_axis=0, concat_axis=0, tiled=True, axis...  32.8 us
    all_to_all x1, starting transfers between devices, exchange(): lax.all_to_all(block, axes, split_axis=0, concat_axis=0, tiled=True, axis...  7.29 us
    pallas_call x1, Pallas kernels, project(): pl.pallas_call(body, out_shape=jax.ShapeDtypeStruct((n_block * len(tiles)...  4.63 us
    ppermute x1, waiting for transfers between devices, on_device(): other_keys = lax.ppermute(keys_out, 'head', pairs)  4.27 us
    pallas_call x1, Pallas kernels, score(): pl.pallas_call(body, out_shape=(pltpu.VMEM((n_rows, 2 * block_len, n_head...  3.51 us
    ppermute x1, starting transfers between devices, on_device(): other_scales = lax.ppermute(scales_out, 'head', pairs)  2.02 us
    ppermute x1, starting transfers between devices, on_device(): other_values = lax.ppermute(values_out, 'head', pairs)  2 us
    pallas_call x1, Pallas kernels, prepare(): pl.pallas_call(body, out_shape=(pltpu.HBM((count, half, width), queries.d...  1.51 us
  transfers between devices with their start and end apart: 4, of which 3 were waited for; matrix products, arithmetic and copies ran while one was open for 3% of the time, Pallas kernels for 7%

profile of v5, /device:TPU:0, one launch (start us, length us, event | category | flops | bytes accessed | tf_op | source)
XLA Modules:
  0.0 64.0 jit_solution(8496370450243095674)
XLA Ops:
  0.0 1.5 %prepare.1 = (bf16[8,4,2048]{2,1,0:T(4,128)(2,1)}, bf16[4,32,1024]{2,1,0:T(8,128)(2,1)S(1)}, bf16[4,32,1024]{2,1,0:T(8,128)(2,1)S(1)}, f32[4,2,8,32]{3,2,1,0:T(8,128)S(1)}) custom-call(s32[1]{0:T(128)} %bitcast.4.own_ref, bf16[8,2048]{1,0:T(8,128)(2,1)} %q_hbm.1, bf16[8,2,32,1024]{3,2,1,0:T(8,128)(2,1)} %refs_1_.1, f32[8,2,8,32]{3,2,1,0:T(8,128)} %refs_2_.1), custom_call_target="tpu_custom_call" | custom-call | tf_op jit(solution)/shard_map/prepare/pallas_call | solution.py:75
  1.5 7.3 %all-to-all-start = ((bf16[8,4,2048]{2,1,0:T(4,128)(2,1)}), bf16[8,4,2048]{2,1,0:T(4,128)(2,1)S(1)}, u32[]{:S(2)}, u32[]{:S(2)}) async-start(bf16[8,4,2048]{2,1,0:T(4,128)(2,1)} %get-tuple-element.17), calls=%async_computation | async-start | bytes 262144 | tf_op jit(solution)/shard_map/all_to_all | solution.py:432
  8.8 2.0 %collective-permute-start.1 = (f32[4,2,8,32]{3,2,1,0:T(8,128)S(1)}, f32[4,2,8,32]{3,2,1,0:T(8,128)S(1)}, u32[]{:S(2)}, u32[]{:S(2)}) collective-permute-start(f32[4,2,8,32]{3,2,1,0:T(8,128)S(1)} %get-tuple-element.22), channel_id=1, source_target_pairs={{0,2},{2,0},{4,6},{6,4},{8,10},{10,8},{12,14},{14,12},{1,3},{3,1},... | collective-permute-start | bytes 24584 | tf_op jit(solution)/shard_map/ppermute | solution.py:477
  10.8 0.0 collective-permute-start
  10.9 2.0 %collective-permute-start.2 = (bf16[4,32,1024]{2,1,0:T(8,128)(2,1)S(1)}, bf16[4,32,1024]{2,1,0:T(8,128)(2,1)S(1)}, u32[]{:S(2)}, u32[]{:S(2)}) collective-permute-start(bf16[4,32,1024]{2,1,0:T(8,128)(2,1)S(1)} %get-tuple-element.25), channel_id=1, source_target_pairs={{0,2},{2,0},{4,6},{6,4},{8,10},{10,8},{12,14},{14,12},{1,3},{3,1},... | collective-permute-start | bytes 786440 | tf_op jit(solution)/shard_map/ppermute | solution.py:479
  12.9 0.7 %dynamic-slice_convert_fusion = f32[4]{0:T(128)S(1)} fusion(s32[8]{0:T(128)} %param.11, s32[]{:T(128)S(6)} %select_n.16), kind=kLoop, calls=%fused_computation.5 | loop fusion | flops 4 | bytes 36 | tf_op jit(solution)/shard_map/convert_element_type | solution.py:42
  13.6 0.1 fusion
  13.7 0.1 pad_maximum_fusion
  13.8 0.7 %dynamic_slice.6 = s32[4]{0:T(128)S(1)} dynamic-slice(s32[8]{0:T(128)} %param.12, s32[]{:T(128)S(6)} %select_n.16), dynamic_slice_sizes={4} | dynamic-slice | bytes 36 | tf_op jit(solution)/shard_map/dynamic_slice | solution.py:470
  14.5 1.1 %stage.1 = (bf16[4,2,1024]{2,1,0:T(2,128)(2,1)S(1)}, bf16[4,2,32,1024]{3,2,1,0:T(8,128)(2,1)S(1)}, f32[4,2,8,32]{3,2,1,0:T(8,128)S(1)}) custom-call(s32[1]{0:T(128)} %bitcast.4.own_ref, bf16[8,2,1024]{2,1,0:T(2,128)(2,1)} %refs_0_.1, bf16[8,2,32,1024]{3,2,1,0:T(8,128)(2,1)} %refs_1_.1, f32[8,2,8,32]{3,2,1,0:T(8,128)} %refs_2_.1), custom_call_target="tpu_custom_call" | custom-call | tf_op jit(solution)/shard_map/stage/pallas_call | solution.py:111
  15.6 0.1 concatenate.9.s_ref
  15.7 0.0 collective-permute-done.1.other_sc
  15.7 0.5 all-to-all-done.q_ref
  16.3 4.3 %collective-permute-done.other_ref = bf16[4,32,1024]{2,1,0:T(8,128)(2,1)S(1)} collective-permute-done((bf16[4,32,1024]{2,1,0:T(8,128)(2,1)S(1)}, bf16[4,32,1024]{2,1,0:T(8,128)(2,1)S(1)}, u32[]{:S(2)}, u32[]{:S(2)}) %collective-permute-start) | collective-permute-done | bytes 262176 | tf_op jit(solution)/shard_map/ppermute | solution.py:476
  20.5 0.0 copy-start
  20.5 0.0 copy-start.1
  20.5 3.5 %score.1 = (f32[4,64,128]{2,1,0:T(8,128)S(1)}, f32[4,8,128]{2,1,0:T(8,128)S(1)}, bf16[3,2048,512]{2,1,0:T(8,128)(2,1)S(1)}) custom-call(s32[8]{0:T(128)S(1)} %concatenate.9.s_ref, bf16[8,4,2048]{2,1,0:T(4,128)(2,1)S(1)} %all-to-all-done.q_ref, f32[4,128]{1,0:T(4,128)S(1)} %get-tuple-element.32.cos_ref, f32[4,128]{1,0:T(4,128)S(1)} %get-tuple-element.33.sin_ref, ...), custom_call_target="tpu_custom_call" | custom-call | tf_op jit(solution)/shard_map/score/pallas_call | solution.py:223
  24.1 1.0 %collective-permute-done.2.other_ref = bf16[4,32,1024]{2,1,0:T(8,128)(2,1)S(1)} collective-permute-done((bf16[4,32,1024]{2,1,0:T(8,128)(2,1)S(1)}, bf16[4,32,1024]{2,1,0:T(8,128)(2,1)S(1)}, u32[]{:S(2)}, u32[]{:S(2)}) %collective-permute-start.2) | collective-permute-done | bytes 262176 | tf_op jit(solution)/shard_map/ppermute | solution.py:479
  25.1 0.6 blend.1
  25.6 10.6 %all_to_all.20.main_ref.stat_ref = bf16[4,136,128]{2,1,0:T(8,128)(2,1)S(1)} all-to-all(bf16[4,136,128]{2,1,0:T(8,128)(2,1)S(1)} %blend.1), channel_id=1, replica_groups={{0,4,8,12},{2,6,10,14},{1,5,9,13},{3,7,11,15},{16,20,24,28},{18,22,26,3..., dimensions={0} | all-to-all | bytes 278528 | tf_op jit(solution)/shard_map/all_to_all | solution.py:432
  36.3 0.3 settle.1
  36.5 10.2 %all_to_all.21.x_ref = bf16[32,16,128]{2,1,0:T(8,128)(2,1)S(1)} all-to-all(bf16[32,16,128]{2,1,0:T(8,128)(2,1)S(1)} %settle.1), channel_id=1, replica_groups=mesh['group'=2,'head'=8,'dp'=2] {'group','head','dp'}, dimensions={0} | all-to-all | bytes 262144 | tf_op jit(solution)/shard_map/all_to_all | solution.py:432
  46.7 4.6 %project.1 = bf16[32,8,512]{2,1,0:T(8,128)(2,1)S(1)} custom-call(s32[1]{0:T(128)} %bitcast.own_ref, bf16[32,16,128]{2,1,0:T(8,128)(2,1)S(1)} %all_to_all.21.x_ref, bf16[3,2048,512]{2,1,0:T(8,128)(2,1)S(1)} %get-tuple-element.28.early_ref, bf16[2048,16384]{1,0:T(8,128)(2,1)} %wo_ref.3), custom_call_target="tpu_custom_call" | custom-call | tf_op jit(solution)/shard_map/project/pallas_call | solution.py:382
  51.4 12.0 %all_to_all.22.share_ref = bf16[32,8,512]{2,1,0:T(8,128)(2,1)S(1)} all-to-all(bf16[32,8,512]{2,1,0:T(8,128)(2,1)S(1)} %project.1), channel_id=1, replica_groups=mesh['group'=2,'head'=8,'dp'=2] {'group','head','dp'}, dimensions={0} | all-to-all | bytes 524288 | tf_op jit(solution)/shard_map/all_to_all | solution.py:432
  63.4 0.0 copy-done
  63.4 0.0 copy-done.1
  63.4 0.7 %finish.1 = bf16[8,2048]{1,0:T(8,128)(2,1)} custom-call(bf16[32,8,512]{2,1,0:T(8,128)(2,1)S(1)} %all_to_all.22.share_ref, f32[1,2048]{1,0:T(1,128)S(1)} %bitcast.6, bf16[8,2048]{1,0:T(8,128)(2,1)S(1)} %copy-done), custom_call_target="tpu_custom_call" | custom-call | tf_op jit(solution)/shard_map/finish/pallas_call | solution.py:420
  (1 shorter events, 0.0 us)
Async XLA Ops:
  1.5 14.7 %all-to-all-start = ((bf16[8,4,2048]{2,1,0:T(4,128)(2,1)}), bf16[8,4,2048]{2,1,0:T(4,128)(2,1)S(1)}, u32[]{:S(2)}, u32[]{:S(2)}) async-start(bf16[8,4,2048]{2,1,0:T(4,128)(2,1)} %get-tuple-element.17), calls=%async_computation | async-start | bytes 262144 | tf_op jit(solution)/shard_map/all_to_all | solution.py:432
  8.8 6.9 %collective-permute-start.1 = (f32[4,2,8,32]{3,2,1,0:T(8,128)S(1)}, f32[4,2,8,32]{3,2,1,0:T(8,128)S(1)}, u32[]{:S(2)}, u32[]{:S(2)}) collective-permute-start(f32[4,2,8,32]{3,2,1,0:T(8,128)S(1)} %get-tuple-element.22), channel_id=1, source_target_pairs={{0,2},{2,0},{4,6},{6,4},{8,10},{10,8},{12,14},{14,12},{1,3},{3,1},... | collective-permute-start | bytes 24584 | tf_op jit(solution)/shard_map/ppermute | solution.py:477
  10.8 9.7 %collective-permute-start = (bf16[4,32,1024]{2,1,0:T(8,128)(2,1)S(1)}, bf16[4,32,1024]{2,1,0:T(8,128)(2,1)S(1)}, u32[]{:S(2)}, u32[]{:S(2)}) collective-permute-start(bf16[4,32,1024]{2,1,0:T(8,128)(2,1)S(1)} %get-tuple-element.20), channel_id=1, source_target_pairs={{0,2},{2,0},{4,6},{6,4},{8,10},{10,8},{12,14},{14,12},{1,3},{3,1},... | collective-permute-start | bytes 786440 | tf_op jit(solution)/shard_map/ppermute | solution.py:476
  10.9 14.2 %collective-permute-start.2 = (bf16[4,32,1024]{2,1,0:T(8,128)(2,1)S(1)}, bf16[4,32,1024]{2,1,0:T(8,128)(2,1)S(1)}, u32[]{:S(2)}, u32[]{:S(2)}) collective-permute-start(bf16[4,32,1024]{2,1,0:T(8,128)(2,1)S(1)} %get-tuple-element.25), channel_id=1, source_target_pairs={{0,2},{2,0},{4,6},{6,4},{8,10},{10,8},{12,14},{14,12},{1,3},{3,1},... | collective-permute-start | bytes 786440 | tf_op jit(solution)/shard_map/ppermute | solution.py:479
  20.5 42.8 %copy-start = (bf16[8,2048]{1,0:T(8,128)(2,1)S(1)}, bf16[8,2048]{1,0:T(8,128)(2,1)}, u32[]{:S(2)}) copy-start(bf16[8,2048]{1,0:T(8,128)(2,1)} %res_ref.1) | copy-start | bytes 98308
  20.5 42.8 %copy-start.1 = (f32[2048]{0:T(1024)S(1)}, f32[2048]{0:T(1024)}, u32[]{:S(2)}) copy-start(f32[2048]{0:T(1024)} %param.16) | copy-start | bytes 24580
